TPU v7x, 32 devices: a whole 2x2x4 slice. The times are simulated.
32 devices in a mesh: dp: 16 (over z, y, core), tensor: 2 (over x).
Axes of the slice: x: 2, y: 2, z: 4, core: 2. Of those that a mesh axis runs over, the one named last changes fastest.
Arguments:
- inputs: bfloat16 [8192, 2048], P(('dp', 'tensor')), may hold values from -6 to 6
- ln_gain: bfloat16 [2048], P('dp'), may hold values from 0.5 to 1.5
- ln_bias: bfloat16 [2048], P('dp'), may hold values from -3 to 3
- qkv_weight: bfloat16 [3, 2048, 2048], P(None, 'dp', 'tensor'), may hold values from -0.125 to 0.125
- out_weight: bfloat16 [2048, 2048], P('dp', 'tensor'), may hold values from -0.75 to 0.75
- fc1_weight: bfloat16 [2048, 8192], P('dp', 'tensor'), may hold values from -0.125 to 0.125
- fc2_weight: bfloat16 [2048, 8192], P('dp', 'tensor'), may hold values from -0.0625 to 0.0625
- cotangent: bfloat16 [8192, 2048], P(('dp', 'tensor')), may hold values from -6 to 6
- m_gain: float32 [2048], P('dp'), may hold values from -78 to 78
- v_gain: float32 [2048], P('dp'), may hold values from 250 to 2500
- m_bias: float32 [2048], P('dp'), may hold values from -78 to 78
- v_bias: float32 [2048], P('dp'), may hold values from 250 to 2500
- m_qkv: float32 [3, 2048, 2048], P(None, 'dp', 'tensor'), may hold values from -9 to 9
- v_qkv: float32 [3, 2048, 2048], P(None, 'dp', 'tensor'), may hold values from 3 to 30
- m_out: float32 [2048, 2048], P('dp', 'tensor'), may hold values from -18 to 18
- v_out: float32 [2048, 2048], P('dp', 'tensor'), may hold values from 10 to 100
- m_fc1: float32 [2048, 8192], P('dp', 'tensor'), may hold values from -24 to 24
- v_fc1: float32 [2048, 8192], P('dp', 'tensor'), may hold values from 25 to 250
- m_fc2: float32 [2048, 8192], P('dp', 'tensor'), may hold values from -48 to 48
- v_fc2: float32 [2048, 8192], P('dp', 'tensor'), may hold values from 80 to 800
Outputs:
- output: bfloat16 [8192, 2048], P(('dp', 'tensor'))
- input_grad: float32 [8192, 2048], P(('dp', 'tensor'))
- gain_grad: float32 [2048], P('dp')
- gain_update: float32 [2048], P('dp')
- gain_m: float32 [2048], P('dp')
- gain_v: float32 [2048], P('dp')
- bias_grad: float32 [2048], P('dp')
- bias_update: float32 [2048], P('dp')
- bias_m: float32 [2048], P('dp')
- bias_v: float32 [2048], P('dp')
- qkv_grad: float32 [3, 2048, 2048], P(None, 'dp', 'tensor')
- qkv_update: float32 [3, 2048, 2048], P(None, 'dp', 'tensor')
- qkv_m: float32 [3, 2048, 2048], P(None, 'dp', 'tensor')
- qkv_v: float32 [3, 2048, 2048], P(None, 'dp', 'tensor')
- out_grad: float32 [2048, 2048], P('dp', 'tensor')
- out_update: float32 [2048, 2048], P('dp', 'tensor')
- out_m: float32 [2048, 2048], P('dp', 'tensor')
- out_v: float32 [2048, 2048], P('dp', 'tensor')
- fc1_grad: float32 [2048, 8192], P('dp', 'tensor')
- fc1_update: float32 [2048, 8192], P('dp', 'tensor')
- fc1_m: float32 [2048, 8192], P('dp', 'tensor')
- fc1_v: float32 [2048, 8192], P('dp', 'tensor')
- fc2_grad: float32 [2048, 8192], P('dp', 'tensor')
- fc2_update: float32 [2048, 8192], P('dp', 'tensor')
- fc2_m: float32 [2048, 8192], P('dp', 'tensor')
- fc2_v: float32 [2048, 8192], P('dp', 'tensor')
All inputs are finite; a program needn't handle non-finite values.
Results may differ from a plain program's by a relative error of at most 0.0085.
The roundings to bfloat16 on the way count: a program that leaves them out, or rounds other values in their place, can miss the bound.
Values may be sent and summed in bfloat16 or wider, within the bound.
No kernel may reach another device: no remote copies, remote signals or barrier semaphores. Data moves between devices by JAX's collectives and lax.ppermute only.
A program may use at most 320 MiB of HBM per device.

v0:
```python
import jax
import jax.numpy as jnp
from jax import lax
from jax.sharding import PartitionSpec as P

HEAD = 64
ROT = 32


EPS_NORM = 1e-05
MASK_FILL = -1e30
BETA_ONE = 0.9
BETA_TWO = 0.95
ADAM_EPS = 1e-08
RATE = 0.02
DECAY = 0.1
STEP_COUNT = 10


def rope_angles(length):
    position = jnp.arange(length, dtype=jnp.float32)[:, None]
    inverse = 10000.0 ** (-(jnp.arange(ROT // 2, dtype=jnp.float32) * 2.0 / ROT))
    angles = position * inverse[None, :]
    return (jnp.cos(angles), jnp.sin(angles))


def rotate(tensor_in, cosine, sine_table):
    half_rot = ROT // 2
    first_half = tensor_in[..., :half_rot]
    second_half = tensor_in[..., half_rot:ROT]
    cos_wide = cosine[:, None, :]
    sin_wide = sine_table[:, None, :]
    return jnp.concatenate(
        [
            first_half * cos_wide - second_half * sin_wide,
            second_half * cos_wide + first_half * sin_wide,
            tensor_in[..., ROT:],
        ],
        axis=-1,
    )


def rotate_back(gradient, cosine, sine_table):
    half_rot = ROT // 2
    upper_part = gradient[..., :half_rot]
    lower_part = gradient[..., half_rot:ROT]
    cos_wide = cosine[:, None, :]
    sin_wide = sine_table[:, None, :]
    return jnp.concatenate(
        [
            upper_part * cos_wide + lower_part * sin_wide,
            lower_part * cos_wide - upper_part * sin_wide,
            gradient[..., ROT:],
        ],
        axis=-1,
    )


def gelu_tanh(values_in):
    return jax.nn.gelu(values_in, approximate=True)


def block_scores(query_rot, key_rot, first_row, block_rows, score_scale):
    scores = (
        jnp.einsum("qhd,khd->hqk", query_rot, key_rot, preferred_element_type=jnp.float32)
        * score_scale
    )
    row_index = first_row + jnp.arange(block_rows, dtype=jnp.int32)[:, None]
    col_index = jnp.arange(key_rot.shape[0], dtype=jnp.int32)[None, :]
    return (query_rot, jnp.where((col_index <= row_index)[None], scores, MASK_FILL))


def adamw(weight, gradient, moment, second):
    new_m = BETA_ONE * moment + (1.0 - BETA_ONE) * gradient
    new_v = BETA_TWO * second + (1.0 - BETA_TWO) * gradient * gradient
    m_hat = new_m / (1.0 - BETA_ONE**STEP_COUNT)
    v_hat = new_v / (1.0 - BETA_TWO**STEP_COUNT)
    update = -RATE * (m_hat / (jnp.sqrt(v_hat) + ADAM_EPS) + DECAY * weight.astype(jnp.float32))
    return (gradient, update, new_m, new_v)


def shards(
    inputs,
    ln_gain,
    ln_bias,
    qkv_weight,
    out_weight,
    fc1_weight,
    fc2_weight,
    cotangent,
    m_gain,
    v_gain,
    m_bias,
    v_bias,
    m_qkv,
    v_qkv,
    m_out,
    v_out,
    m_fc1,
    v_fc1,
    m_fc2,
    v_fc2,
):
    qkv_full, out_full, fc1_full, fc2_full, gain_full, bias_full = (
        lax.all_gather(qkv_weight, "dp", axis=1, tiled=True),
        lax.all_gather(out_weight, "dp", axis=0, tiled=True),
        lax.all_gather(fc1_weight, "dp", axis=0, tiled=True),
        lax.all_gather(fc2_weight, "dp", axis=0, tiled=True),
        lax.all_gather(ln_gain, "dp", axis=0, tiled=True),
        lax.all_gather(ln_bias, "dp", axis=0, tiled=True),
    )
    gain_wide = gain_full.astype(jnp.float32)
    bias_wide = bias_full.astype(jnp.float32)
    own_rows = inputs.astype(jnp.float32)
    centred = own_rows - jnp.mean(own_rows, axis=1, keepdims=True)
    inv_std = lax.rsqrt(jnp.mean(centred * centred, axis=1, keepdims=True) + EPS_NORM)
    normed = centred * inv_std
    hidden_own = (normed * gain_wide + bias_wide).astype(jnp.bfloat16)
    hidden = lax.all_gather(hidden_own, "tensor", axis=0, tiled=True)
    length = hidden.shape[0]
    width_local = qkv_full.shape[2]
    heads_local = width_local // HEAD
    score_scale = HEAD ** (-0.5)
    cosine, sine_table = rope_angles(length)
    projected = jnp.einsum("ld,cde->cle", hidden, qkv_full, preferred_element_type=jnp.float32)
    shaped = projected.reshape(3, length, heads_local, HEAD)
    query_rot = rotate(shaped[0], cosine, sine_table).astype(jnp.bfloat16)
    key_rot = rotate(shaped[1], cosine, sine_table).astype(jnp.bfloat16)
    values = shaped[2].astype(jnp.bfloat16)
    block_rows = min(512, length)
    count_blocks = length // block_rows
    starts = jnp.arange(count_blocks, dtype=jnp.int32) * block_rows

    def forward_block(first_row):
        query_block, scores = block_scores(query_rot, key_rot, first_row, block_rows, score_scale)
        row_max = jnp.max(scores, axis=2, keepdims=True)
        raw_exp = jnp.exp(scores - row_max)
        row_total = jnp.sum(raw_exp, axis=2, keepdims=True)
        softmax = (raw_exp / row_total).astype(jnp.bfloat16)
        ctx_block = jnp.einsum("hqk,khd->qhd", softmax, values, preferred_element_type=jnp.float32)
        return (ctx_block.astype(jnp.bfloat16), (row_max + jnp.log(row_total))[..., 0])

    contexts, log_totals = lax.map(forward_block, starts)
    context = contexts.reshape(length, width_local)
    attn_part = jnp.einsum("le,de->ld", context, out_full, preferred_element_type=jnp.float32)
    pre_act = jnp.dot(hidden, fc1_full, preferred_element_type=jnp.float32)
    activated = gelu_tanh(pre_act).astype(jnp.bfloat16)
    mlp_part = jnp.einsum("lf,df->ld", activated, fc2_full, preferred_element_type=jnp.float32)
    summed = lax.psum_scatter(attn_part + mlp_part, "tensor", scatter_dimension=0, tiled=True)
    output = (own_rows + summed).astype(jnp.bfloat16)
    qkv_back, out_back, fc1_back, fc2_back = (
        lax.all_gather(qkv_weight, "dp", axis=1, tiled=True),
        lax.all_gather(out_weight, "dp", axis=0, tiled=True),
        lax.all_gather(fc1_weight, "dp", axis=0, tiled=True),
        lax.all_gather(fc2_weight, "dp", axis=0, tiled=True),
    )
    cotan_full = lax.all_gather(cotangent, "tensor", axis=0, tiled=True)
    d_act = jnp.dot(cotan_full, fc2_back, preferred_element_type=jnp.float32)
    ignored, pull_back = jax.vjp(gelu_tanh, pre_act)
    d_pre = pull_back(d_act)[0].astype(jnp.bfloat16)
    d_hidden_mlp = jnp.einsum("lf,df->ld", d_pre, fc1_back, preferred_element_type=jnp.float32)
    d_context = jnp.dot(cotan_full, out_back, preferred_element_type=jnp.float32).astype(
        jnp.bfloat16
    )
    d_context = d_context.reshape(length, heads_local, HEAD)

    def backward_block(running, block_item):
        first_row, log_total = block_item
        d_keys, d_values = running
        query_block, scores = block_scores(query_rot, key_rot, first_row, block_rows, score_scale)
        softmax = jnp.exp(scores - log_total[:, :, None])
        d_soft = jnp.einsum("qhd,khd->hqk", d_context, values, preferred_element_type=jnp.float32)
        centre = jnp.sum(d_soft * softmax, axis=2, keepdims=True)
        d_scores = (softmax * (d_soft - centre)).astype(jnp.bfloat16)
        d_query = (
            jnp.einsum("hqk,khd->qhd", d_scores, key_rot, preferred_element_type=jnp.float32)
            * score_scale
        )
        d_keys = (
            d_keys
            + jnp.einsum("hqk,qhd->khd", d_scores, query_block, preferred_element_type=jnp.float32)
            * score_scale
        )
        d_values = d_values + jnp.einsum(
            "hqk,qhd->khd",
            softmax.astype(jnp.bfloat16),
            d_context,
            preferred_element_type=jnp.float32,
        )
        return ((d_keys, d_values), d_query)

    empty = jnp.zeros((length, heads_local, HEAD), jnp.float32)
    (d_keys, d_values), d_queries = lax.scan(backward_block, (empty, empty), (starts, log_totals))
    d_queries = d_queries.reshape(length, heads_local, HEAD)
    d_proj = (
        jnp.stack(
            [
                rotate_back(d_queries, cosine, sine_table),
                rotate_back(d_keys, cosine, sine_table),
                d_values,
            ]
        )
        .reshape(3, length, width_local)
        .astype(jnp.bfloat16)
    )
    qkv_part = jnp.einsum("ld,cle->cde", hidden, d_proj, preferred_element_type=jnp.float32)
    d_hidden_attn = jnp.einsum("cle,cde->ld", d_proj, qkv_back, preferred_element_type=jnp.float32)
    d_hidden = lax.psum_scatter(
        d_hidden_attn + d_hidden_mlp, "tensor", scatter_dimension=0, tiled=True
    )
    gain_part = jnp.sum(d_hidden * normed, axis=0)
    bias_part = jnp.sum(d_hidden, axis=0)
    scaled_grad = d_hidden * gain_wide
    input_grad = cotangent.astype(jnp.float32) + inv_std * (
        scaled_grad
        - jnp.mean(scaled_grad, axis=1, keepdims=True)
        - normed * jnp.mean(scaled_grad * normed, axis=1, keepdims=True)
    )
    fc2_part = jnp.einsum("ld,lf->df", cotan_full, activated, preferred_element_type=jnp.float32)
    fc1_part = jnp.einsum("ld,lf->df", hidden, d_pre, preferred_element_type=jnp.float32)
    out_part = jnp.einsum("ld,le->de", cotan_full, context, preferred_element_type=jnp.float32)
    qkv_grad, out_grad, fc1_grad, fc2_grad, gain_half, bias_half = (
        lax.psum_scatter(qkv_part, "dp", scatter_dimension=1, tiled=True),
        lax.psum_scatter(out_part, "dp", scatter_dimension=0, tiled=True),
        lax.psum_scatter(fc1_part, "dp", scatter_dimension=0, tiled=True),
        lax.psum_scatter(fc2_part, "dp", scatter_dimension=0, tiled=True),
        lax.psum_scatter(gain_part, "dp", scatter_dimension=0, tiled=True),
        lax.psum_scatter(bias_part, "dp", scatter_dimension=0, tiled=True),
    )
    gain_grad, bias_grad = lax.psum((gain_half, bias_half), "tensor")
    gain_res = adamw(ln_gain, gain_grad, m_gain, v_gain)
    bias_res = adamw(ln_bias, bias_grad, m_bias, v_bias)
    qkv_res = adamw(qkv_weight, qkv_grad, m_qkv, v_qkv)
    out_res = adamw(out_weight, out_grad, m_out, v_out)
    fc1_res = adamw(fc1_weight, fc1_grad, m_fc1, v_fc1)
    fc2_res = adamw(fc2_weight, fc2_grad, m_fc2, v_fc2)
    return (
        output,
        input_grad,
        gain_res[0],
        gain_res[1],
        gain_res[2],
        gain_res[3],
        bias_res[0],
        bias_res[1],
        bias_res[2],
        bias_res[3],
        qkv_res[0],
        qkv_res[1],
        qkv_res[2],
        qkv_res[3],
        out_res[0],
        out_res[1],
        out_res[2],
        out_res[3],
        fc1_res[0],
        fc1_res[1],
        fc1_res[2],
        fc1_res[3],
        fc2_res[0],
        fc2_res[1],
        fc2_res[2],
        fc2_res[3],
    )


def solution(mesh):
    return jax.shard_map(
        shards,
        mesh=mesh,
        in_specs=(
            P(("dp", "tensor"), None),
            P("dp"),
            P("dp"),
            P(None, "dp", "tensor"),
            P("dp", "tensor"),
            P("dp", "tensor"),
            P("dp", "tensor"),
            P(("dp", "tensor"), None),
            P("dp"),
            P("dp"),
            P("dp"),
            P("dp"),
            P(None, "dp", "tensor"),
            P(None, "dp", "tensor"),
            P("dp", "tensor"),
            P("dp", "tensor"),
            P("dp", "tensor"),
            P("dp", "tensor"),
            P("dp", "tensor"),
            P("dp", "tensor"),
        ),
        out_specs=(
            P(("dp", "tensor"), None),
            P(("dp", "tensor"), None),
            P("dp"),
            P("dp"),
            P("dp"),
            P("dp"),
            P("dp"),
            P("dp"),
            P("dp"),
            P("dp"),
            P(None, "dp", "tensor"),
            P(None, "dp", "tensor"),
            P(None, "dp", "tensor"),
            P(None, "dp", "tensor"),
            P("dp", "tensor"),
            P("dp", "tensor"),
            P("dp", "tensor"),
            P("dp", "tensor"),
            P("dp", "tensor"),
            P("dp", "tensor"),
            P("dp", "tensor"),
            P("dp", "tensor"),
            P("dp", "tensor"),
            P("dp", "tensor"),
            P("dp", "tensor"),
            P("dp", "tensor"),
        ),
        check_vma=False,
    )
```

profile of v0, /device:TPU:0, one launch (start us, length us, event | category | flops | bytes accessed | tf_op | source)
XLA Modules:
  0.0 1644.1 jit_solution(8891050419869749501)
XLA Ops:
  8.7 23.2 %all-gather = bf16[16,1,128]{2,1,0:T(2,128)(2,1)S(1)} all-gather(bf16[1,1,128]{2,1,0:T(2,128)(2,1)} %bitcast.78), channel_id=1, replica_groups=mesh['dp'=16,'tensor'=2] {'dp'}, dimensions={0}, use_global_device_ids=true | all-gather | bytes 4352 | tf_op jit(solution)/shard_map/all_gather | solution.py:109
  31.9 17.5 %all-gather.1 = bf16[16,1,128]{2,1,0:T(2,128)(2,1)S(1)} all-gather(bf16[1,1,128]{2,1,0:T(2,128)(2,1)} %bitcast.77), channel_id=1, replica_groups=mesh['dp'=16,'tensor'=2] {'dp'}, dimensions={0}, use_global_device_ids=true | all-gather | bytes 4352 | tf_op jit(solution)/shard_map/all_gather | solution.py:110
  55.0 43.2 %all-gather.13.cloned.1.call-done = bf16[2048,1024]{1,0:T(8,128)(2,1)} async-done(((bf16[128,1024]{1,0:T(8,128)(2,1)}), bf16[2048,1024]{1,0:T(8,128)(2,1)}) %all-gather.13.cloned.1.call-update) | async-done | bytes 4194320 | tf_op jit(solution)/shard_map/all_gather | solution.py:106
  104.1 27.9 %all-gather.9.cloned.1.call-done = bf16[512,2048]{1,0:T(8,128)(2,1)} async-done(((bf16[256,2048]{1,0:T(8,128)(2,1)}), bf16[512,2048]{1,0:T(8,128)(2,1)}) %all-gather.9.cloned.1.call-update) | async-done | bytes 2097168 | tf_op jit(solution)/shard_map/all_gather | solution.py:119
  132.0 102.9 %all-gather.11.cloned.1.call-done = bf16[3,2048,1024]{2,1,0:T(8,128)(2,1)} async-done(((bf16[3,128,1024]{2,1,0:T(8,128)(2,1)}), bf16[3,2048,1024]{2,1,0:T(8,128)(2,1)}) %all-gather.11.cloned.1.call-update) | async-done | bytes 12582928 | tf_op jit(solution)/shard_map/all_gather | solution.py:105
  234.8 9.9 convolution_bitcast_fusion.3
  291.4 15.0 multiply_reduce_fusion
  308.4 10.6 multiply_convert_fusion
  330.4 9.6 fusion.34
  341.3 11.4 fusion.37
  352.7 9.2 all-gather.17.cloned.1.call-done
  362.0 15.0 fusion.57
  376.9 112.1 %all-gather.15.cloned.1.call-done = bf16[2048,4096]{1,0:T(8,128)(2,1)} async-done(((bf16[128,4096]{1,0:T(8,128)(2,1)}), bf16[2048,4096]{1,0:T(8,128)(2,1)}) %all-gather.15.cloned.1.call-update) | async-done | bytes 16777232 | tf_op jit(solution)/shard_map/all_gather | solution.py:107
  489.1 20.4 %fusion.8 = (bf16[512,4096]{1,0:T(8,128)(2,1)S(1)}, f32[512,4096]{1,0:T(8,128)}) fusion(f32[512,4096]{1,0:T(8,128)} %fusion.57, bf16[512,2048]{1,0:T(8,128)(2,1)S(1)} %copy-done.10, bf16[2048,4096]{1,0:T(8,128)(2,1)} %all-gather.15.cloned.1.call-done), kind=kOutput, calls=%fused_computation.18 | convolution fusion | flops 8631877632 | bytes 39845888 | tf_op jit(solution)/shard_map/dot_general | solution.py:146
  511.6 14.9 bitcast_add_fusion
  533.4 18.5 %convolution_add_fusion = f32[512,2048]{1,0:T(8,128)} fusion(f32[512,2048]{1,0:T(8,128)} %fusion.56, bf16[2048,4096]{1,0:T(8,128)(2,1)} %all-gather.17.cloned.1.call-done, f32[512,4096]{1,0:T(8,128)} %get-tuple-element.198), kind=kOutput, calls=%fused_computation.25 | convolution fusion | flops 8609857536 | bytes 33554432 | tf_op jit(solution)/shard_map/lf,df->ld/dot_general | solution.py:148
  551.9 13.6 convolution_bitcast_fusion.1
  565.6 17.8 %fusion.58 = f32[2048,4096]{1,0:T(8,128)} fusion(bf16[512,2048]{1,0:T(8,128)(2,1)S(1)} %copy-done.10, bf16[512,4096]{1,0:T(8,128)(2,1)} %copy-done.54), kind=kOutput, calls=%fused_computation.115 | convolution fusion | flops 8589934592 | bytes 39845888 | tf_op jit(solution)/shard_map/ld,lf->df/dot_general | solution.py:220
  585.0 19.9 %convolution_bitcast_fusion = f32[2048,4096]{1,0:T(8,128)} fusion(bf16[512,2048]{1,0:T(8,128)(2,1)S(1)} %copy-done.51, f32[512,4096]{1,0:T(8,128)} %get-tuple-element.198), kind=kOutput, calls=%fused_computation | convolution fusion | flops 8608808960 | bytes 44040192 | tf_op jit(solution)/shard_map/ld,lf->df/dot_general | solution.py:219
  619.7 32.9 %reduce-scatter.9.cloned.1.call-done = f32[256,2048]{1,0:T(8,128)} async-done(((f32[512,2048]{1,0:T(8,128)}), f32[256,2048]{1,0:T(8,128)}) %reduce-scatter.9.cloned.1.call-update) | async-done | bytes 2097168 | tf_op jit(solution)/shard_map/reduce_scatter | solution.py:208
  655.3 61.2 %all-reduce.2 = (f32[2048]{0:T(1024)S(1)}, f32[2048]{0:T(1024)S(1)}) all-reduce(f32[2048]{0:T(1024)S(1)} %get-tuple-element.149, f32[2048]{0:T(1024)S(1)} %get-tuple-element.152), channel_id=4, replica_groups=mesh['dp'=16,'tensor'=2] {'dp'}, use_global_device_ids=true, to_apply=%region_10.11.clone | all-reduce | flops 4096 | bytes 32768
  728.3 228.9 %reduce-scatter.11.cloned.1.call-done = f32[3,128,1024]{1,2,0:T(8,128)} async-done(((f32[3,2048,1024]{1,2,0:T(8,128)}), f32[3,128,1024]{1,2,0:T(8,128)}) %reduce-scatter.11.cloned.1.call-update) | async-done | bytes 1572880 | tf_op jit(solution)/shard_map/reduce_scatter | solution.py:223
  969.9 323.9 %reduce-scatter.15.cloned.1.call-done = f32[128,4096]{1,0:T(8,128)} async-done(((f32[2048,4096]{1,0:T(8,128)}), f32[128,4096]{1,0:T(8,128)}) %reduce-scatter.15.cloned.1.call-update) | async-done | bytes 2097168 | tf_op jit(solution)/shard_map/reduce_scatter | solution.py:225
  1300.6 329.8 %reduce-scatter.17.cloned.1.call-done = f32[128,4096]{1,0:T(8,128)} async-done(((f32[2048,4096]{1,0:T(8,128)}), f32[128,4096]{1,0:T(8,128)}) %reduce-scatter.17.cloned.1.call-update) | async-done | bytes 2097168 | tf_op jit(solution)/shard_map/reduce_scatter | solution.py:226
  (209 shorter events, 139.3 us)
Async XLA Ops:
  7.2 47.7 %all-gather.19.cloned.1.call-start = ((), (), s32[]{:S(2)}) async-start(), calls=%async_computation.12 | async-start | bytes 3145728 | tf_op jit(solution)/shard_map/all_gather | solution.py:157
  7.9 90.3 %all-gather.13.cloned.1.call-start = ((), (), s32[]{:S(2)}) async-start(), calls=%async_computation.8 | async-start | bytes 4456448 | tf_op jit(solution)/shard_map/all_gather | solution.py:106
  8.7 123.3 %all-gather.9.cloned.1.call-start = ((), (), s32[]{:S(2)}) async-start(), calls=%async_computation.6 | async-start | bytes 3145728 | tf_op jit(solution)/shard_map/all_gather | solution.py:119
  52.1 182.7 %all-gather.11.cloned.1.call-start = ((), (), s32[]{:S(2)}) async-start(), calls=%async_computation.7 | async-start | bytes 13369344 | tf_op jit(solution)/shard_map/all_gather | solution.py:105
  52.7 309.3 %all-gather.17.cloned.1.call-start = ((), (), s32[]{:S(2)}) async-start(), calls=%async_computation.10 | async-start | bytes 17825792 | tf_op jit(solution)/shard_map/all_gather | solution.py:108
  53.3 435.8 %all-gather.15.cloned.1.call-start = ((), (), s32[]{:S(2)}) async-start(), calls=%async_computation.9 | async-start | bytes 17825792 | tf_op jit(solution)/shard_map/all_gather | solution.py:107
  53.9 560.3 %reduce-scatter.13.cloned.1.call-start = ((), (), s32[]{:S(2)}) async-start(), calls=%async_computation.15 | async-start | bytes 8912896 | tf_op jit(solution)/shard_map/reduce_scatter | solution.py:224
  54.9 203.9 %copy-start.31 = (f32[512,16]{0,1:T(8,128)}, f32[512,16]{0,1:T(8,128)S(1)}, u32[]{:S(2)}) copy-start(f32[512,16]{0,1:T(8,128)S(1)} %get-tuple-element.191) | copy-start | bytes 98308
  54.9 203.9 %copy-start.33 = (f32[512,16]{0,1:T(8,128)}, f32[512,16]{0,1:T(8,128)S(1)}, u32[]{:S(2)}) copy-start(f32[512,16]{0,1:T(8,128)S(1)} %get-tuple-element.192) | copy-start | bytes 98308
  319.0 333.5 %reduce-scatter.9.cloned.1.call-start = ((), (), s32[]{:S(2)}) async-start(), calls=%async_computation.13 | async-start | bytes 6291456 | tf_op jit(solution)/shard_map/reduce_scatter | solution.py:208
  352.7 136.4 %copy-start.10 = (bf16[512,2048]{1,0:T(8,128)(2,1)S(1)}, bf16[512,2048]{1,0:T(8,128)(2,1)}, u32[]{:S(2)}) copy-start(bf16[512,2048]{1,0:T(8,128)(2,1)} %all-gather.9.cloned.1.call-done) | copy-start | bytes 6291460
  526.5 196.4 %reduce-scatter.7.cloned.1.call-start = ((), (), s32[]{:S(2)}) async-start(), calls=%async_computation.11 | async-start | bytes 6291456 | tf_op jit(solution)/shard_map/reduce_scatter | solution.py:149
  551.9 405.3 %reduce-scatter.11.cloned.1.call-start = ((), (), s32[]{:S(2)}) async-start(), calls=%async_computation.14 | async-start | bytes 26738688 | tf_op jit(solution)/shard_map/reduce_scatter | solution.py:223
  565.5 728.4 %reduce-scatter.15.cloned.1.call-start = ((), (), s32[]{:S(2)}) async-start(), calls=%async_computation.16 | async-start | bytes 35651584 | tf_op jit(solution)/shard_map/reduce_scatter | solution.py:225
  583.4 1046.9 %reduce-scatter.17.cloned.1.call-start = ((), (), s32[]{:S(2)}) async-start(), calls=%async_computation.17 | async-start | bytes 35651584 | tf_op jit(solution)/shard_map/reduce_scatter | solution.py:226
  618.7 103.1 %copy-start.42 = (bf16[128]{0:T(256)(128)(2,1)S(1)}, bf16[128]{0:T(256)(128)(2,1)}, u32[]{:S(2)}) copy-start(bf16[128]{0:T(256)(128)(2,1)} %param.22) | copy-start | bytes 772
  618.7 103.1 %copy-start.44 = (f32[128]{0:T(128)S(1)}, f32[128]{0:T(128)}, u32[]{:S(2)}) copy-start(f32[128]{0:T(128)} %param.30) | copy-start | bytes 1540
  618.7 103.1 %copy-start.45 = (f32[128]{0:T(128)S(1)}, f32[128]{0:T(128)}, u32[]{:S(2)}) copy-start(f32[128]{0:T(128)} %param.31) | copy-start | bytes 1540
  618.7 103.6 %copy-start.43 = (bf16[128]{0:T(256)(128)(2,1)S(1)}, bf16[128]{0:T(256)(128)(2,1)}, u32[]{:S(2)}) copy-start(bf16[128]{0:T(256)(128)(2,1)} %param.21) | copy-start | bytes 772
  618.7 103.6 %copy-start.46 = (f32[128]{0:T(128)S(1)}, f32[128]{0:T(128)}, u32[]{:S(2)}) copy-start(f32[128]{0:T(128)} %param.28) | copy-start | bytes 1540
  618.7 103.6 %copy-start.47 = (f32[128]{0:T(128)S(1)}, f32[128]{0:T(128)}, u32[]{:S(2)}) copy-start(f32[128]{0:T(128)} %param.29) | copy-start | bytes 1540
  652.6 70.3 %copy-start.3 = (f32[256,2048]{1,0:T(8,128)S(1)}, f32[256,2048]{1,0:T(8,128)}, u32[]{:S(2)}) copy-start(f32[256,2048]{1,0:T(8,128)} %reduce-scatter.9.cloned.1.call-done) | copy-start | bytes 6291460
  968.3 325.6 %copy-start.7 = (bf16[128,4096]{1,0:T(8,128)(2,1)S(1)}, bf16[128,4096]{1,0:T(8,128)(2,1)}, u32[]{:S(2)}) copy-start(bf16[128,4096]{1,0:T(8,128)(2,1)} %param.25) | copy-start | bytes 3145732
  969.9 660.4 %copy-start.8 = (bf16[128,4096]{1,0:T(8,128)(2,1)S(1)}, bf16[128,4096]{1,0:T(8,128)(2,1)}, u32[]{:S(2)}) copy-start(bf16[128,4096]{1,0:T(8,128)(2,1)} %param.26) | copy-start | bytes 3145732
  (47 other events, 418.3 us)
Sparse Core Ops, SparseCore 0:
  9.6 35.7 all-gather.18
  47.6 50.5 all-gather.12
  100.3 31.5 all-gather.8
  134.0 100.7 all-gather.10
  236.8 125.0 all-gather.16
  364.0 125.0 all-gather.14
  493.1 103.0 reduce-scatter.12
  598.5 54.0 reduce-scatter.8
  655.0 54.3 reduce-scatter.6
  713.3 243.8 reduce-scatter.10
  962.0 331.8 reduce-scatter.14
  1298.6 331.7 reduce-scatter.16
where the time goes:
time: 1650 us; the launch traced here: 1640 us
  waiting for transfers between devices  1210 us (73%)
  matrix products  206 us (12%)
  blocking collectives  107 us (6%)
  other arithmetic  53.8 us (3%)
  local copies, waits for them, and re-layouts  47 us (3%)
    reduce_scatter x1, waiting for transfers between devices, shards(): lax.psum_scatter(fc2_part, 'dp', scatter_dimension=0, tiled=True)  330 us
    reduce_scatter x1, waiting for transfers between devices, shards(): lax.psum_scatter(fc1_part, 'dp', scatter_dimension=0, tiled=True)  324 us
    reduce_scatter x1, waiting for transfers between devices, shards(): lax.psum_scatter(qkv_part, 'dp', scatter_dimension=1, tiled=True)  229 us
    all_gather x1, waiting for transfers between devices, shards(): lax.all_gather(fc1_weight, 'dp', axis=0, tiled=True)  112 us
    all_gather x1, waiting for transfers between devices, shards(): lax.all_gather(qkv_weight, 'dp', axis=1, tiled=True)  103 us
    unnamed x1, blocking collectives  61.2 us
    all_gather x1, waiting for transfers between devices, shards(): lax.all_gather(out_weight, 'dp', axis=0, tiled=True)  43.2 us
  transfers between devices with their start and end apart: 12, of which 9 were waited for; matrix products, arithmetic and copies ran while one was open for 18% of the time, Pallas kernels for 0%

commit v1 on v0

v1 whole, which is shorter than its diff:
```python
import jax
import jax.numpy as jnp
import numpy as np
from jax import lax
from jax.experimental import pallas as pl
from jax.experimental.pallas import tpu as pltpu
from jax.sharding import Mesh
from jax.sharding import PartitionSpec as P

HEAD = 64
ROT = 32
PAIR = 2 * HEAD
SCALE = HEAD ** (-0.5)

EPS_NORM = 1e-05
MASK_FILL = -1e30
BETA_ONE = 0.9
BETA_TWO = 0.95
ADAM_EPS = 1e-08
RATE = 0.02
DECAY = 0.1
STEP_COUNT = 10

BF16 = jnp.bfloat16
F32 = jnp.float32


def swap(value, axis):
    return lax.ppermute(value, axis, [(0, 1), (1, 0)])


def swap_inner(value, flip):
    return lax.ppermute(value, ("y", "c"), [(i, i ^ flip) for i in range(4)])


def inner_index():
    return 2 * lax.axis_index("y") + lax.axis_index("c")


def spread_columns(weight):
    r = inner_index()
    rows, width = weight.shape[0], weight.shape[1] // 4
    out = jnp.zeros((4 * rows, width), weight.dtype)
    for flip in range(4):
        piece = lax.dynamic_slice(weight, (0, (r ^ flip) * width), (rows, width))
        if flip:
            piece = swap_inner(piece, flip)
        out = lax.dynamic_update_slice(out, piece, ((r ^ flip) * rows, 0))
    return out


def spread_qkv(weight):
    r = inner_index()
    rows, width = weight.shape[1], weight.shape[2] // 4
    out = jnp.zeros((4 * rows, 3 * width), weight.dtype)
    for flip in range(4):
        piece = lax.dynamic_slice(weight, (0, 0, (r ^ flip) * width), (3, rows, width))
        piece = jnp.concatenate([piece[0], piece[1], piece[2]], axis=1)
        if flip:
            piece = swap_inner(piece, flip)
        out = lax.dynamic_update_slice(out, piece, ((r ^ flip) * rows, 0))
    return out


def collect_columns(part):
    r = inner_index()
    rows = part.shape[0] // 4
    pieces = []
    for flip in range(4):
        piece = lax.dynamic_slice(part, ((r ^ flip) * rows, 0), (rows, part.shape[1]))
        if flip:
            piece = swap_inner(piece.astype(BF16), flip).astype(F32)
        pieces.append(piece)
    return r, pieces


def join_columns(part):
    r, pieces = collect_columns(part)
    rows, width = pieces[0].shape
    out = jnp.zeros((rows, 4 * width), F32)
    for flip, piece in enumerate(pieces):
        out = lax.dynamic_update_slice(out, piece, (0, (r ^ flip) * width))
    return out


def join_qkv(part):
    r, pieces = collect_columns(part)
    rows, width = pieces[0].shape[0], pieces[0].shape[1] // 3
    out = jnp.zeros((3, rows, 4 * width), F32)
    for flip, piece in enumerate(pieces):
        piece = jnp.stack([piece[:, i * width : (i + 1) * width] for i in range(3)])
        out = lax.dynamic_update_slice(out, piece, (0, 0, (r ^ flip) * width))
    return out


def gather_outer(value):
    return lax.all_gather(value, "o", axis=0, tiled=True)


def reduce_outer(part):
    n = lax.axis_size("o")
    z = lax.axis_index("o")
    rows = part.shape[0] // n

    def block(i):
        return lax.dynamic_slice(part, (i * rows, 0), (rows, part.shape[1]))

    up = down = None
    for s in range(n - 1, 0, -1):
        to_up = block(jnp.minimum(z + s, n - 1))
        to_down = block(jnp.maximum(z - s, 0))
        if up is not None:
            to_up = to_up + up
            to_down = to_down + down
        up = lax.ppermute(to_up, "o", [(i, i + 1) for i in range(0, n - s)])
        down = lax.ppermute(to_down, "o", [(i + 1, i) for i in range(s - 1, n - 1)])
    return block(z).astype(F32) + up.astype(F32) + down.astype(F32)


def order_halves(own, other):
    first = lax.axis_index("t") == 0
    return jnp.concatenate([jnp.where(first, own, other), jnp.where(first, other, own)])


def gather_plane(own):
    mid = own.shape[0] // 2
    by_t = swap(own, "t")
    by_y = swap(own, "y")
    corner = jnp.concatenate([swap(by_t[:mid], "y"), swap(by_y[mid:], "t")])
    core = jnp.concatenate([order_halves(own, by_t), order_halves(by_y, corner)])
    return jnp.concatenate([core, swap(core, "c")])


def scatter_plane(part):
    rows = part.shape[0] // 8
    mid = rows // 2
    core = part[: 4 * rows] + swap(part[4 * rows :], "c")
    t = lax.axis_index("t")

    def block(sequence, half):
        return lax.dynamic_slice(core, ((2 * sequence + half) * rows, 0), (rows, part.shape[1]))

    own, by_t, by_y, corner = block(0, t), block(0, 1 - t), block(1, t), block(1, 1 - t)
    by_t = jnp.concatenate([by_t[:mid] + swap(corner[:mid], "y"), by_t[mid:]])
    by_y = jnp.concatenate([by_y[:mid], by_y[mid:] + swap(corner[mid:], "t")])
    return own.astype(F32) + swap(by_t, "t").astype(F32) + swap(by_y, "y").astype(F32)


def flips_outer(value):
    n = lax.axis_size("o")
    bit = 1
    while bit < n:
        value = value + lax.ppermute(value, "o", [(i, i ^ bit) for i in range(n)])
        bit *= 2
    return value


def gather_vectors(pair):
    count = 4 * lax.axis_size("o")
    index = 4 * lax.axis_index("o") + inner_index()
    out = jnp.zeros((2, count * pair.shape[1]), pair.dtype)
    out = lax.dynamic_update_slice(out, pair, (0, index * pair.shape[1]))
    out = out + swap(out, "c")
    out = out + swap(out, "y")
    return flips_outer(out)


def sum_vectors(pair):
    pair = pair + swap(pair, "c")
    pair = pair + swap(pair, "t")
    pair = pair + swap(pair, "y")
    pair = flips_outer(pair)
    count = 4 * lax.axis_size("o")
    index = 4 * lax.axis_index("o") + inner_index()
    width = pair.shape[1] // count
    return lax.dynamic_slice(pair, (0, index * width), (2, width))


def lane_tables(length):
    position = np.arange(length, dtype=np.float32)[:, None]
    inverse = 10000.0 ** (-(np.arange(ROT // 2, dtype=np.float32) * 2.0 / ROT))
    angles = (position * inverse.astype(np.float32)[None, :]).astype(np.float64)
    cosine = jnp.asarray(np.cos(angles).astype(np.float32))
    sine = jnp.asarray(np.sin(angles).astype(np.float32))
    none = jnp.zeros_like(sine)
    rest = jnp.zeros((length, HEAD - ROT), F32)
    tables = (
        jnp.concatenate([cosine, cosine, rest + 1.0], axis=1),
        jnp.concatenate([sine, none, rest], axis=1),
        jnp.concatenate([none, sine, rest], axis=1),
    )
    return tuple(jnp.concatenate([table, table], axis=1) for table in tables)


def attention_body(proj_ref, grad_ref, cos_ref, low_ref, high_ref, context_ref, d_proj_ref):
    length, width = grad_ref.shape
    half = length // 2
    cosine, low, high = cos_ref[...], low_ref[...], high_ref[...]
    first = lax.broadcasted_iota(jnp.int32, (length, PAIR), 1) < HEAD
    row = lax.broadcasted_iota(jnp.int32, (half, half), 0)
    col = lax.broadcasted_iota(jnp.int32, (half, half), 1)
    keep = row <= col

    def turn(value, sign):
        ahead = pltpu.roll(value, PAIR - ROT // 2, 1)
        behind = pltpu.roll(value, ROT // 2, 1)
        return value * cosine - sign * ahead * low + sign * behind * high

    def rows_by_rows(a, b):
        return lax.dot_general(a, b, (((1,), (1,)), ((), ())), preferred_element_type=F32)

    def turned(a, b):
        return lax.dot_general(a, b, (((0,), (0,)), ((), ())), preferred_element_type=F32)

    def plain(a, b):
        return lax.dot_general(a, b, (((1,), (0,)), ((), ())), preferred_element_type=F32)

    def over_keys(function, value):
        return function(value, axis=0, keepdims=True)

    for pair in range(width // PAIR):
        lanes = pl.ds(pair * PAIR, PAIR)
        key_lanes = pl.ds(width + pair * PAIR, PAIR)
        value_lanes = pl.ds(2 * width + pair * PAIR, PAIR)
        query = (turn(proj_ref[:, lanes], 1.0).astype(BF16).astype(F32) * SCALE).astype(BF16)
        keys = turn(proj_ref[:, key_lanes], 1.0).astype(BF16)
        values = proj_ref[:, value_lanes].astype(BF16)
        grad = grad_ref[:, lanes]
        context = jnp.zeros((length, PAIR), F32)
        d_query = context
        d_keys_a = d_keys_b = d_values_a = d_values_b = jnp.zeros((half, PAIR), F32)
        for head in range(2):
            mine = first if head == 0 else jnp.logical_not(first)
            q, k, v, g = (
                jnp.where(mine, item, jnp.zeros_like(item)) for item in (query, keys, values, grad)
            )
            qa, qb, ga, gb = q[:half], q[half:], g[:half], g[half:]
            s_aa = jnp.where(keep, rows_by_rows(keys[:half], qa), MASK_FILL)
            s_ab = rows_by_rows(keys[:half], qb)
            s_bb = jnp.where(keep, rows_by_rows(keys[half:], qb), MASK_FILL)
            max_a = over_keys(jnp.max, s_aa)
            max_b = jnp.maximum(over_keys(jnp.max, s_ab), over_keys(jnp.max, s_bb))
            e_aa, e_ab, e_bb = jnp.exp(s_aa - max_a), jnp.exp(s_ab - max_b), jnp.exp(s_bb - max_b)
            inv_a = 1.0 / over_keys(jnp.sum, e_aa)
            inv_b = 1.0 / (over_keys(jnp.sum, e_ab) + over_keys(jnp.sum, e_bb))
            p_aa, p_ab, p_bb = e_aa * inv_a, e_ab * inv_b, e_bb * inv_b
            r_aa, r_ab, r_bb = p_aa.astype(BF16), p_ab.astype(BF16), p_bb.astype(BF16)
            d_aa = rows_by_rows(values[:half], ga)
            d_ab = rows_by_rows(values[:half], gb)
            d_bb = rows_by_rows(values[half:], gb)
            centre_a = over_keys(jnp.sum, d_aa * p_aa)
            centre_b = over_keys(jnp.sum, d_ab * p_ab) + over_keys(jnp.sum, d_bb * p_bb)
            t_aa = (p_aa * (d_aa - centre_a)).astype(BF16)
            t_ab = (p_ab * (d_ab - centre_b)).astype(BF16)
            t_bb = (p_bb * (d_bb - centre_b)).astype(BF16)
            context += jnp.concatenate(
                [turned(r_aa, v[:half]), turned(r_ab, v[:half]) + turned(r_bb, v[half:])]
            )
            d_query += jnp.concatenate(
                [turned(t_aa, k[:half]), turned(t_ab, k[:half]) + turned(t_bb, k[half:])]
            )
            d_keys_a += plain(t_aa, qa) + plain(t_ab, qb)
            d_keys_b += plain(t_bb, qb)
            d_values_a += plain(r_aa, ga) + plain(r_ab, gb)
            d_values_b += plain(r_bb, gb)
        context_ref[:, lanes] = context.astype(BF16)
        d_proj_ref[:, lanes] = turn(d_query * SCALE, -1.0).astype(BF16)
        d_keys = jnp.concatenate([d_keys_a, d_keys_b])
        d_proj_ref[:, key_lanes] = turn(d_keys, -1.0).astype(BF16)
        d_proj_ref[:, value_lanes] = jnp.concatenate([d_values_a, d_values_b]).astype(BF16)


def attention(proj, d_context, length):
    tokens, width = d_context.shape
    table = pl.BlockSpec((length, PAIR), lambda s: (0, 0))
    one = pl.BlockSpec((length, width), lambda s: (s, 0))
    three = pl.BlockSpec((length, 3 * width), lambda s: (s, 0))
    return pl.pallas_call(
        attention_body,
        out_shape=(
            jax.ShapeDtypeStruct((tokens, width), BF16),
            jax.ShapeDtypeStruct((tokens, 3 * width), BF16),
        ),
        grid=(tokens // length,),
        in_specs=[three, one, table, table, table],
        out_specs=(one, three),
        compiler_params=pltpu.CompilerParams(vmem_limit_bytes=48 << 20),
        name="attention",
    )(proj, d_context, *lane_tables(length))


def gelu_tanh(values_in):
    return jax.nn.gelu(values_in, approximate=True)


def adamw(weight, gradient, moment, second):
    new_m = BETA_ONE * moment + (1.0 - BETA_ONE) * gradient
    new_v = BETA_TWO * second + (1.0 - BETA_TWO) * gradient * gradient
    m_hat = new_m / (1.0 - BETA_ONE**STEP_COUNT)
    v_hat = new_v / (1.0 - BETA_TWO**STEP_COUNT)
    update = -RATE * (m_hat / (jnp.sqrt(v_hat) + ADAM_EPS) + DECAY * weight.astype(F32))
    return (gradient, update, new_m, new_v)


def dot_nn(a, b):
    return lax.dot_general(a, b, (((1,), (0,)), ((), ())), preferred_element_type=F32)


def dot_nt(a, b):
    return lax.dot_general(a, b, (((1,), (1,)), ((), ())), preferred_element_type=F32)


def dot_tn(a, b):
    return lax.dot_general(a, b, (((0,), (0,)), ((), ())), preferred_element_type=F32)


def shards(
    inputs,
    ln_gain,
    ln_bias,
    qkv_weight,
    out_weight,
    fc1_weight,
    fc2_weight,
    cotangent,
    m_gain,
    v_gain,
    m_bias,
    v_bias,
    m_qkv,
    v_qkv,
    m_out,
    v_out,
    m_fc1,
    v_fc1,
    m_fc2,
    v_fc2,
):
    length = 2 * inputs.shape[0]
    qkv_cols = gather_outer(spread_qkv(qkv_weight))
    out_cols = gather_outer(spread_columns(out_weight))
    fc1_cols = gather_outer(spread_columns(fc1_weight))
    fc2_cols = gather_outer(spread_columns(fc2_weight))

    vectors = gather_vectors(jnp.stack([ln_gain, ln_bias])).astype(F32)
    gain_wide, bias_wide = vectors[0], vectors[1]
    own_rows = inputs.astype(F32)
    centred = own_rows - jnp.mean(own_rows, axis=1, keepdims=True)
    inv_std = lax.rsqrt(jnp.mean(centred * centred, axis=1, keepdims=True) + EPS_NORM)
    normed = centred * inv_std
    hidden_own = (normed * gain_wide + bias_wide).astype(BF16)
    hidden = gather_plane(hidden_own)
    cotan = gather_plane(cotangent)

    proj = dot_nn(hidden, qkv_cols)
    d_context = dot_nn(cotan, out_cols).astype(BF16)
    context, d_proj = attention(proj, d_context, length)
    qkv_sum = reduce_outer(dot_tn(hidden, d_proj).astype(BF16))
    out_sum = reduce_outer(dot_tn(cotan, context).astype(BF16))

    pre_act = dot_nn(hidden, fc1_cols)
    activated = gelu_tanh(pre_act).astype(BF16)
    fc2_sum = reduce_outer(dot_tn(cotan, activated).astype(BF16))
    d_act = dot_nn(cotan, fc2_cols)
    ignored, pull_back = jax.vjp(gelu_tanh, pre_act)
    d_pre = pull_back(d_act)[0].astype(BF16)
    fc1_sum = reduce_outer(dot_tn(hidden, d_pre).astype(BF16))

    branch = dot_nt(context, out_cols) + dot_nt(activated, fc2_cols)
    output = (own_rows + scatter_plane(branch.astype(BF16))).astype(BF16)
    d_hidden = scatter_plane((dot_nt(d_proj, qkv_cols) + dot_nt(d_pre, fc1_cols)).astype(BF16))

    vector_parts = jnp.stack([jnp.sum(d_hidden * normed, axis=0), jnp.sum(d_hidden, axis=0)])
    vector_grads = sum_vectors(vector_parts)
    scaled_grad = d_hidden * gain_wide
    input_grad = cotangent.astype(F32) + inv_std * (
        scaled_grad
        - jnp.mean(scaled_grad, axis=1, keepdims=True)
        - normed * jnp.mean(scaled_grad * normed, axis=1, keepdims=True)
    )
    gain_res = adamw(ln_gain, vector_grads[0], m_gain, v_gain)
    bias_res = adamw(ln_bias, vector_grads[1], m_bias, v_bias)
    qkv_res = adamw(qkv_weight, join_qkv(qkv_sum), m_qkv, v_qkv)
    out_res = adamw(out_weight, join_columns(out_sum), m_out, v_out)
    fc1_res = adamw(fc1_weight, join_columns(fc1_sum), m_fc1, v_fc1)
    fc2_res = adamw(fc2_weight, join_columns(fc2_sum), m_fc2, v_fc2)
    return (
        output,
        input_grad,
        *gain_res,
        *bias_res,
        *qkv_res,
        *out_res,
        *fc1_res,
        *fc2_res,
    )


def solution(mesh):
    dp, tensor = mesh.devices.shape
    inner = Mesh(mesh.devices.reshape(dp // 4, 2, 2, tensor), ("o", "y", "c", "t"))
    rows = P(("o", "y", "c", "t"), None)
    vector = P(("o", "y", "c"))
    stack = P(None, ("o", "y", "c"), "t")
    matrix = P(("o", "y", "c"), "t")
    return jax.shard_map(
        shards,
        mesh=inner,
        in_specs=(rows, vector, vector, stack, matrix, matrix, matrix, rows)
        + (vector,) * 4
        + (stack,) * 2
        + (matrix,) * 6,
        out_specs=(rows, rows) + (vector,) * 8 + (stack,) * 4 + (matrix,) * 12,
        check_vma=False,
    )
```

time: 1650 us -> 752 us (0.46)
  waiting for transfers between devices: 1210 us -> 277 us
  starting transfers between devices: 0.48 us -> 165 us
  blocking collectives: 107 us -> 0 us
  matrix products: 206 us -> 146 us
  other arithmetic: 53.8 us -> 71.6 us
  Pallas kernels: 0 us -> 17.1 us
    reduce_scatter x6 -> x0, waiting for transfers between devices: 915 us -> none  [the longest x1 330 us: shards(): lax.psum_scatter(fc2_part, 'dp', scatter_dimension=0, tiled=True)]
    all_gather x6 -> x4, waiting for transfers between devices: 295 us -> 75.1 us  [gather_outer(): return lax.all_gather(value, 'o', axis=0, tiled=True)]
    ppermute x0 -> x77, waiting for transfers between devices: none -> 202 us  [the longest x25 71.6 us: swap(): return lax.ppermute(value, axis, [(0, 1), (1, 0)])]
    ppermute x0 -> x77, starting transfers between devices: none -> 165 us  [the longest x12 89.9 us: reduce_outer(): up = lax.ppermute(to_up, 'o', [(i, i + 1) for i in range(0, n - s)])]
    unnamed x1 -> x0, blocking collectives: 61.2 us -> none
    dot_general x18 -> x12, matrix products: 206 us -> 146 us  [the longest x4 54.7 us: dot_nt(): lax.dot_general(a, b, (((1,), (1,)), ((), ())), preferred_element_type=F32)]
    all_gather x2 -> x0, blocking collectives: 40.6 us -> none  [the longest x1 23.2 us: shards(): lax.all_gather(ln_gain, 'dp', axis=0, tiled=True)]
    add x2 -> x33, other arithmetic: 6.08 us -> 33.2 us  [the longest x8 11.2 us: reduce_outer(): to_up = to_up + up]
  transfers between devices with their start and end apart: 12 -> 81, of which waited for: 9 -> 33; matrix products, arithmetic and copies ran while one was open for 18% -> 34% of each run, Pallas kernels for 0% -> 2%
where the time goes in v1:
time: 752 us; the launch traced here: 744 us
  waiting for transfers between devices  277 us (37%)
  starting transfers between devices  165 us (22%)
  matrix products  146 us (19%)
  other arithmetic  71.6 us (10%)
  local copies, waits for them, and re-layouts  52.2 us (7%)
  Pallas kernels  17.1 us (2%)
  between operations  15.6 us (2%)
    ppermute x12, starting transfers between devices, reduce_outer(): up = lax.ppermute(to_up, 'o', [(i, i + 1) for i in range(0, n - s)])  89.9 us
    all_gather x4, waiting for transfers between devices, gather_outer(): return lax.all_gather(value, 'o', axis=0, tiled=True)  75.1 us
    ppermute x25, waiting for transfers between devices, swap(): return lax.ppermute(value, axis, [(0, 1), (1, 0)])  71.6 us
    dot_general x4, matrix products, dot_nt(): lax.dot_general(a, b, (((1,), (1,)), ((), ())), preferred_element_type=F32)  54.7 us
    ppermute x12, waiting for transfers between devices, reduce_outer(): up = lax.ppermute(to_up, 'o', [(i, i + 1) for i in range(0, n - s)])  52.2 us
    dot_general x4, matrix products, dot_nn(): lax.dot_general(a, b, (((1,), (0,)), ((), ())), preferred_element_type=F32)  49 us
    dot_general x4, matrix products, dot_tn(): lax.dot_general(a, b, (((0,), (0,)), ((), ())), preferred_element_type=F32)  42.1 us
    ppermute x12, waiting for transfers between devices, reduce_outer(): down = lax.ppermute(to_down, 'o', [(i + 1, i) for i in range(s - 1, n - 1)])  39.6 us
  transfers between devices with their start and end apart: 81, of which 33 were waited for; matrix products, arithmetic and copies ran while one was open for 34% of the time, Pallas kernels for 2%

profile of v1, /device:TPU:0, one launch (start us, length us, event | category | flops | bytes accessed | tf_op | source)
XLA Modules:
  0.0 744.2 jit_solution(14666033369784814231)
XLA Ops:
  21.6 15.1 %collective-permute-done.1 = bf16[2,2048]{1,0:T(2,128)(2,1)S(1)} collective-permute-done((bf16[2,2048]{1,0:T(2,128)(2,1)S(1)}, bf16[2,2048]{1,0:T(2,128)(2,1)S(1)}, u32[]{:S(2)}, u32[]{:S(2)}) %collective-permute-start.1) | collective-permute-done | bytes 8224 | tf_op jit(solution)/shard_map/ppermute | solution.py:29
  63.9 15.0 %collective-permute-done.5 = bf16[256,2048]{1,0:T(8,128)(2,1)} collective-permute-done((bf16[256,2048]{1,0:T(8,128)(2,1)}, bf16[256,2048]{1,0:T(8,128)(2,1)}, u32[]{:S(2)}, u32[]{:S(2)}) %collective-permute-start.5) | collective-permute-done | bytes 1048608 | tf_op jit(solution)/shard_map/ppermute | solution.py:29
  145.8 12.0 %fusion.39.proj_ref = f32[2048,768]{1,0:T(8,128)} fusion(bf16[2048,2048]{1,0:T(8,128)(2,1)} %constant_dynamic-update-slice_fusion.2, bf16[2048,768]{1,0:T(8,128)(2,1)} %all-gather.5.cloned.1.call-done), kind=kOutput, calls=%fused_computation.230 | convolution fusion | flops 6442450944 | bytes 17825792 | tf_op jit(solution)/shard_map/dot_general | solution.py:306
  157.9 17.1 %attention.1 = (bf16[2048,256]{1,0:T(8,128)(2,1)S(1)}, bf16[2048,768]{1,0:T(8,128)(2,1)S(1)}) custom-call(f32[2048,768]{1,0:T(8,128)} %fusion.39.proj_ref, bf16[2048,256]{1,0:T(8,128)(2,1)S(1)} %convolution_convert_fusion.4.grad_ref, f32[512,128]{1,0:T(8,128)S(1)} %copy-done.2, f32[512,128]{1,0:T(8,128)S(1)} %copy-done.1, f32[512,128]{1,0:T(8,128)S(1)} %copy-done), custom_call_target="tpu_custom_call" | custom-call | tf_op jit(solution)/shard_map/attention/pallas_call | solution.py:278
  188.7 9.0 %collective-permute-done.50 = bf16[512,256]{1,0:T(8,128)(2,1)S(1)} collective-permute-done((bf16[512,256]{1,0:T(8,128)(2,1)S(1)}, bf16[512,256]{1,0:T(8,128)(2,1)S(1)}, u32[]{:S(2)}, u32[]{:S(2)}) %collective-permute-start.50) | collective-permute-done | bytes 262176 | tf_op jit(solution)/shard_map/ppermute | solution.py:115
  202.1 10.5 %convolution_convert_fusion.2 = bf16[2048,768]{1,0:T(8,128)(2,1)S(1)} fusion(bf16[2048,2048]{1,0:T(8,128)(2,1)} %constant_dynamic-update-slice_fusion.2, bf16[2048,768]{1,0:T(8,128)(2,1)} %copy-done.3), kind=kOutput, calls=%fused_computation.18 | convolution fusion | flops 6444023808 | bytes 14680064 | tf_op jit(solution)/shard_map/dot_general | solution.py:314
  223.8 18.2 %all-gather.9.cloned.1.call-done = bf16[2048,1024]{1,0:T(8,128)(2,1)} async-done(((bf16[512,1024]{1,0:T(8,128)(2,1)}), bf16[2048,1024]{1,0:T(8,128)(2,1)}) %all-gather.9.cloned.1.call-update) | async-done | bytes 4194320 | tf_op jit(solution)/shard_map/all_gather | solution.py:97
  242.0 12.5 %fusion.40 = f32[2048,1024]{1,0:T(8,128)S(1)} fusion(bf16[2048,2048]{1,0:T(8,128)(2,1)} %constant_dynamic-update-slice_fusion.2, bf16[2048,1024]{1,0:T(8,128)(2,1)} %all-gather.9.cloned.1.call-done), kind=kOutput, calls=%fused_computation.231 | convolution fusion | flops 8589934592 | bytes 20971520 | tf_op jit(solution)/shard_map/dot_general | solution.py:306
  257.8 13.2 %convolution_convert_fusion = bf16[2048,1024]{1,0:T(8,128)(2,1)} fusion(bf16[2048,2048]{1,0:T(8,128)(2,1)} %constant_dynamic-update-slice_fusion.9, f32[2048,1024]{1,0:T(8,128)S(1)} %fusion.40), kind=kOutput, calls=%fused_computation.16 | convolution fusion | flops 8610906112 | bytes 20971520 | tf_op jit(solution)/shard_map/dot_general | solution.py:314
  271.0 56.9 %all-gather.11.cloned.1.call-done = bf16[2048,1024]{1,0:T(8,128)(2,1)} async-done(((bf16[512,1024]{1,0:T(8,128)(2,1)}), bf16[2048,1024]{1,0:T(8,128)(2,1)}) %all-gather.11.cloned.1.call-update) | async-done | bytes 4194320 | tf_op jit(solution)/shard_map/all_gather | solution.py:97
  327.9 18.5 %fusion.6 = bf16[2048,1024]{1,0:T(8,128)(2,1)S(1)} fusion(f32[2048,1024]{1,0:T(8,128)} %copy-done.53, bf16[2048,2048]{1,0:T(8,128)(2,1)} %constant_dynamic-update-slice_fusion.9, bf16[2048,1024]{1,0:T(8,128)(2,1)} %all-gather.11.cloned.1.call-done), kind=kOutput, calls=%fused_computation.10 | convolution fusion | flops 8631877632 | bytes 25165824 | tf_op jit(solution)/shard_map/dot_general | solution.py:306
  346.4 11.4 %convolution_convert_fusion.1 = bf16[2048,1024]{1,0:T(8,128)(2,1)S(1)} fusion(bf16[2048,2048]{1,0:T(8,128)(2,1)} %constant_dynamic-update-slice_fusion.2, bf16[2048,1024]{1,0:T(8,128)(2,1)S(1)} %fusion.6), kind=kOutput, calls=%fused_computation.17 | convolution fusion | flops 8592031744 | bytes 16777216 | tf_op jit(solution)/shard_map/dot_general | solution.py:314
  365.1 11.9 %fusion.41 = f32[2048,2048]{1,0:T(8,128)} fusion(bf16[2048,1024]{1,0:T(8,128)(2,1)S(1)} %fusion.6, bf16[2048,1024]{1,0:T(8,128)(2,1)S(1)} %copy-done.52), kind=kOutput, calls=%fused_computation.232 | convolution fusion | flops 8589934592 | bytes 25165824 | tf_op jit(solution)/shard_map/dot_general | solution.py:310
  377.0 13.3 %add_convert_fusion = bf16[2048,2048]{1,0:T(8,128)(2,1)} fusion(f32[2048,2048]{1,0:T(8,128)} %fusion.41, bf16[2048,768]{1,0:T(8,128)(2,1)S(1)} %copy-done.4, bf16[2048,768]{1,0:T(8,128)(2,1)} %all-gather.5.cloned.1.call-done), kind=kOutput, calls=%fused_computation | convolution fusion | flops 6450839552 | bytes 31457280 | tf_op jit(solution)/shard_map/dot_general | solution.py:310
  390.3 18.1 %fusion.31 = f32[2048,2048]{1,0:T(8,128)} fusion(bf16[2048,1024]{1,0:T(8,128)(2,1)} %all-gather.11.cloned.1.call-done, f32[2048,1024]{1,0:T(8,128)} %copy-done.53), kind=kOutput, calls=%fused_computation.228 | convolution fusion | flops 8608808960 | bytes 29360128 | tf_op jit(solution)/shard_map/dot_general | solution.py:310
  416.5 11.4 %add_convert_fusion.1 = bf16[2048,2048]{1,0:T(8,128)(2,1)} fusion(f32[2048,2048]{1,0:T(8,128)} %fusion.31, bf16[2048,256]{1,0:T(8,128)(2,1)S(1)} %get-tuple-element.28, bf16[2048,256]{1,0:T(8,128)(2,1)S(1)} %copy-done.33), kind=kOutput, calls=%fused_computation.1 | convolution fusion | flops 2155872256 | bytes 27262976 | tf_op jit(solution)/shard_map/dot_general | solution.py:310
  457.4 11.9 %collective-permute-done.69 = bf16[512,1024]{1,0:T(8,128)(2,1)S(1)} collective-permute-done((bf16[512,1024]{1,0:T(8,128)(2,1)S(1)}, bf16[512,1024]{1,0:T(8,128)(2,1)S(1)}, u32[]{:S(2)}, u32[]{:S(2)}) %collective-permute-start.69) | collective-permute-done | bytes 1048608 | tf_op jit(solution)/shard_map/ppermute | solution.py:115
  471.5 19.2 %collective-permute-done.60 = bf16[512,1024]{1,0:T(8,128)(2,1)S(1)} collective-permute-done((bf16[512,1024]{1,0:T(8,128)(2,1)S(1)}, bf16[512,1024]{1,0:T(8,128)(2,1)S(1)}, u32[]{:S(2)}, u32[]{:S(2)}) %collective-permute-start.60) | collective-permute-done | bytes 1048608 | tf_op jit(solution)/shard_map/ppermute | solution.py:115
  501.4 12.1 %collective-permute-done.43 = bf16[512,768]{1,0:T(8,128)(2,1)S(1)} collective-permute-done((bf16[512,768]{1,0:T(8,128)(2,1)S(1)}, bf16[512,768]{1,0:T(8,128)(2,1)S(1)}, u32[]{:S(2)}, u32[]{:S(2)}) %collective-permute-start.43) | collective-permute-done | bytes 786464 | tf_op jit(solution)/shard_map/ppermute | solution.py:115
  539.0 48.8 %collective-permute-start.61 = (bf16[512,1024]{1,0:T(8,128)(2,1)}, bf16[512,1024]{1,0:T(8,128)(2,1)}, u32[]{:S(2)}, u32[]{:S(2)}) collective-permute-start(bf16[512,1024]{1,0:T(8,128)(2,1)} %get-tuple-element.73), channel_id=1, source_target_pairs={{0,8},{8,16},{16,24},{1,9},{9,17},{17,25},{2,10},{10,18},{18,26},{... | collective-permute-start | bytes 3145736 | tf_op jit(solution)/shard_map/ppermute | solution.py:115
  609.9 9.2 %collective-permute-done.32 = bf16[128,2048]{1,0:T(8,128)(2,1)S(1)} collective-permute-done((bf16[128,2048]{1,0:T(8,128)(2,1)S(1)}, bf16[128,2048]{1,0:T(8,128)(2,1)S(1)}, u32[]{:S(2)}, u32[]{:S(2)}) %collective-permute-start.32) | collective-permute-done | bytes 524320 | tf_op jit(solution)/shard_map/ppermute | solution.py:29
  634.2 28.1 %collective-permute-done.64 = bf16[512,1024]{1,0:T(8,128)(2,1)S(1)} collective-permute-done((bf16[512,1024]{1,0:T(8,128)(2,1)S(1)}, bf16[512,1024]{1,0:T(8,128)(2,1)S(1)}, u32[]{:S(2)}, u32[]{:S(2)}) %collective-permute-start.64) | collective-permute-done | bytes 1048608 | tf_op jit(solution)/shard_map/ppermute | solution.py:116
  685.0 13.7 %collective-permute-done.33 = bf16[256,2048]{1,0:T(8,128)(2,1)S(1)} collective-permute-done((bf16[256,2048]{1,0:T(8,128)(2,1)}, bf16[256,2048]{1,0:T(8,128)(2,1)S(1)}, u32[]{:S(2)}, u32[]{:S(2)}) %collective-permute-start.33) | collective-permute-done | bytes 1048608 | tf_op jit(solution)/shard_map/ppermute | solution.py:29
  710.8 16.1 %collective-permute-start.39 = (f32[2,2048]{1,0:T(2,128)S(1)}, f32[2,2048]{1,0:T(2,128)S(1)}, u32[]{:S(2)}, u32[]{:S(2)}) collective-permute-start(f32[2,2048]{1,0:T(2,128)S(1)} %add.498), channel_id=1, source_target_pairs={{0,8},{8,0},{16,24},{24,16},{1,9},{9,1},{17,25},{25,17},{2,10},{10... | collective-permute-start | bytes 49160 | tf_op jit(solution)/shard_map/ppermute | solution.py:153
  (405 shorter events, 305.5 us)
Async XLA Ops:
  7.2 127.7 %all-gather.7.cloned.1.call-start = ((), (), s32[]{:S(2)}) async-start(), calls=%async_computation.1 | async-start | bytes 1310720 | tf_op jit(solution)/shard_map/all_gather | solution.py:97
  7.3 51.7 %collective-permute-start.12 = (bf16[256,2048]{1,0:T(8,128)(2,1)}, bf16[256,2048]{1,0:T(8,128)(2,1)}, u32[]{:S(2)}, u32[]{:S(2)}) collective-permute-start(bf16[256,2048]{1,0:T(8,128)(2,1)} %param.29), channel_id=1, source_target_pairs={{0,1},{1,0},{2,3},{3,2},{4,5},{5,4},{6,7},{7,6},{8,9},{9,8},{10,11... | collective-permute-start | bytes 3145736 | tf_op jit(solution)/shard_map/ppermute | solution.py:29
  10.3 50.3 %collective-permute-start.13 = (bf16[256,2048]{1,0:T(8,128)(2,1)}, bf16[256,2048]{1,0:T(8,128)(2,1)S(1)}, u32[]{:S(2)}, u32[]{:S(2)}) collective-permute-start(bf16[256,2048]{1,0:T(8,128)(2,1)} %param.29), channel_id=1, source_target_pairs={{0,4},{4,0},{1,5},{5,1},{2,6},{6,2},{3,7},{7,3},{8,12},{12,8},{9,1... | collective-permute-start | bytes 3145736 | tf_op jit(solution)/shard_map/ppermute | solution.py:29
  50.5 95.4 %all-gather.5.cloned.1.call-start = ((), (), s32[]{:S(2)}) async-start(), calls=%async_computation | async-start | bytes 3932160 | tf_op jit(solution)/shard_map/all_gather | solution.py:97
  59.0 183.0 %all-gather.9.cloned.1.call-start = ((), (), s32[]{:S(2)}) async-start(), calls=%async_computation.2 | async-start | bytes 5242880 | tf_op jit(solution)/shard_map/all_gather | solution.py:97
  125.6 202.3 %all-gather.11.cloned.1.call-start = ((), (), s32[]{:S(2)}) async-start(), calls=%async_computation.3 | async-start | bytes 5242880 | tf_op jit(solution)/shard_map/all_gather | solution.py:97
  127.9 60.0 %collective-permute-start.25 = (bf16[128,1024]{1,0:T(8,128)(2,1)}, bf16[128,1024]{1,0:T(8,128)(2,1)S(1)}, u32[]{:S(2)}, u32[]{:S(2)}) collective-permute-start(bf16[128,1024]{1,0:T(8,128)(2,1)} %get-tuple-element.109), channel_id=1, source_target_pairs={{0,6},{2,4},{4,2},{6,0},{1,7},{3,5},{5,3},{7,1},{8,14},{10,12},{12... | collective-permute-start | bytes 786440 | tf_op jit(solution)/shard_map/ppermute | solution.py:33
  129.0 58.2 %collective-permute-start.24 = (bf16[128,1024]{1,0:T(8,128)(2,1)}, bf16[128,1024]{1,0:T(8,128)(2,1)S(1)}, u32[]{:S(2)}, u32[]{:S(2)}) collective-permute-start(bf16[128,1024]{1,0:T(8,128)(2,1)} %get-tuple-element.110), channel_id=1, source_target_pairs={{0,4},{2,6},{4,0},{6,2},{1,5},{3,7},{5,1},{7,3},{8,12},{10,14},{12... | collective-permute-start | bytes 786440 | tf_op jit(solution)/shard_map/ppermute | solution.py:33
  130.2 55.3 %collective-permute-start.23 = (bf16[128,1024]{1,0:T(8,128)(2,1)}, bf16[128,1024]{1,0:T(8,128)(2,1)}, u32[]{:S(2)}, u32[]{:S(2)}) collective-permute-start(bf16[128,1024]{1,0:T(8,128)(2,1)} %get-tuple-element.111), channel_id=1, source_target_pairs={{0,2},{2,0},{4,6},{6,4},{1,3},{3,1},{5,7},{7,5},{8,10},{10,8},{12,... | collective-permute-start | bytes 786440 | tf_op jit(solution)/shard_map/ppermute | solution.py:33
  215.2 194.9 %collective-permute-start.41 = (bf16[512,768]{1,0:T(8,128)(2,1)}, bf16[512,768]{1,0:T(8,128)(2,1)}, u32[]{:S(2)}, u32[]{:S(2)}) collective-permute-start(bf16[512,768]{1,0:T(8,128)(2,1)} %constant_dynamic-slice_fusion.11), channel_id=1, source_target_pairs={{0,8},{1,9},{2,10},{3,11},{4,12},{5,13},{6,14},{7,15}} | collective-permute-start | bytes 2359304 | tf_op jit(solution)/shard_map/ppermute | solution.py:115
  218.9 216.5 %collective-permute-start.52 = (bf16[512,256]{1,0:T(8,128)(2,1)}, bf16[512,256]{1,0:T(8,128)(2,1)S(1)}, u32[]{:S(2)}, u32[]{:S(2)}) collective-permute-start(bf16[512,256]{1,0:T(8,128)(2,1)} %get-tuple-element.101), channel_id=1, source_target_pairs={{0,8},{8,16},{16,24},{1,9},{9,17},{17,25},{2,10},{10,18},{18,26},{... | collective-permute-start | bytes 786440 | tf_op jit(solution)/shard_map/ppermute | solution.py:115
  222.4 185.9 %collective-permute-start.53 = (bf16[512,256]{1,0:T(8,128)(2,1)}, bf16[512,256]{1,0:T(8,128)(2,1)}, u32[]{:S(2)}, u32[]{:S(2)}) collective-permute-start(bf16[512,256]{1,0:T(8,128)(2,1)} %get-tuple-element.102), channel_id=1, source_target_pairs={{24,16},{25,17},{26,18},{27,19},{28,20},{29,21},{30,22},{31,23}} | collective-permute-start | bytes 786440 | tf_op jit(solution)/shard_map/ppermute | solution.py:116
  360.3 78.3 %collective-permute-start.68 = (bf16[512,1024]{1,0:T(8,128)(2,1)}, bf16[512,1024]{1,0:T(8,128)(2,1)}, u32[]{:S(2)}, u32[]{:S(2)}) collective-permute-start(bf16[512,1024]{1,0:T(8,128)(2,1)} %constant_dynamic-slice_fusion.4), channel_id=1, source_target_pairs={{0,8},{1,9},{2,10},{3,11},{4,12},{5,13},{6,14},{7,15}} | collective-permute-start | bytes 3145736 | tf_op jit(solution)/shard_map/ppermute | solution.py:115
  362.8 83.0 %collective-permute-start.59 = (bf16[512,1024]{1,0:T(8,128)(2,1)S(1)}, bf16[512,1024]{1,0:T(8,128)(2,1)}, u32[]{:S(2)}, u32[]{:S(2)}) collective-permute-start(bf16[512,1024]{1,0:T(8,128)(2,1)S(1)} %constant_dynamic-slice_fusion.7), channel_id=1, source_target_pairs={{0,8},{1,9},{2,10},{3,11},{4,12},{5,13},{6,14},{7,15}} | collective-permute-start | bytes 3145736 | tf_op jit(solution)/shard_map/ppermute | solution.py:115
  435.4 156.5 %collective-permute-start.26 = (bf16[1024,2048]{1,0:T(8,128)(2,1)S(1)}, bf16[1024,2048]{1,0:T(8,128)(2,1)}, u32[]{:S(2)}, u32[]{:S(2)}) collective-permute-start(bf16[1024,2048]{1,0:T(8,128)(2,1)S(1)} %slice.199), channel_id=1, source_target_pairs={{0,2},{2,0},{1,3},{3,1},{4,6},{6,4},{5,7},{7,5},{8,10},{10,8},{9,1... | collective-permute-start | bytes 12582920 | tf_op jit(solution)/shard_map/ppermute | solution.py:29
  447.5 43.2 %collective-permute-start.60 = (bf16[512,1024]{1,0:T(8,128)(2,1)S(1)}, bf16[512,1024]{1,0:T(8,128)(2,1)S(1)}, u32[]{:S(2)}, u32[]{:S(2)}) collective-permute-start(bf16[512,1024]{1,0:T(8,128)(2,1)S(1)} %dynamic-slice_add_fusion.6), channel_id=1, source_target_pairs={{0,8},{8,16},{1,9},{9,17},{2,10},{10,18},{3,11},{11,19},{4,12},{12... | collective-permute-start | bytes 3145736 | tf_op jit(solution)/shard_map/ppermute | solution.py:115
  500.6 95.6 %collective-permute-start.31 = (bf16[1024,2048]{1,0:T(8,128)(2,1)}, bf16[1024,2048]{1,0:T(8,128)(2,1)}, u32[]{:S(2)}, u32[]{:S(2)}) collective-permute-start(bf16[1024,2048]{1,0:T(8,128)(2,1)} %slice.201), channel_id=1, source_target_pairs={{0,2},{2,0},{1,3},{3,1},{4,6},{6,4},{5,7},{7,5},{8,10},{10,8},{9,1... | collective-permute-start | bytes 12582920 | tf_op jit(solution)/shard_map/ppermute | solution.py:29
  526.7 97.8 %collective-permute-start.70 = (bf16[512,1024]{1,0:T(8,128)(2,1)}, bf16[512,1024]{1,0:T(8,128)(2,1)}, u32[]{:S(2)}, u32[]{:S(2)}) collective-permute-start(bf16[512,1024]{1,0:T(8,128)(2,1)} %get-tuple-element.71), channel_id=1, source_target_pairs={{0,8},{8,16},{16,24},{1,9},{9,17},{17,25},{2,10},{10,18},{18,26},{... | collective-permute-start | bytes 3145736 | tf_op jit(solution)/shard_map/ppermute | solution.py:115
  532.9 56.3 %collective-permute-start.63 = (bf16[512,1024]{1,0:T(8,128)(2,1)S(1)}, bf16[512,1024]{1,0:T(8,128)(2,1)S(1)}, u32[]{:S(2)}, u32[]{:S(2)}) collective-permute-start(bf16[512,1024]{1,0:T(8,128)(2,1)S(1)} %dynamic-slice_add_fusion.4), channel_id=1, source_target_pairs={{16,8},{24,16},{17,9},{25,17},{18,10},{26,18},{19,11},{27,19},{20,... | collective-permute-start | bytes 3145736 | tf_op jit(solution)/shard_map/ppermute | solution.py:116
  539.0 95.1 %collective-permute-start.61 = (bf16[512,1024]{1,0:T(8,128)(2,1)}, bf16[512,1024]{1,0:T(8,128)(2,1)}, u32[]{:S(2)}, u32[]{:S(2)}) collective-permute-start(bf16[512,1024]{1,0:T(8,128)(2,1)} %get-tuple-element.73), channel_id=1, source_target_pairs={{0,8},{8,16},{16,24},{1,9},{9,17},{17,25},{2,10},{10,18},{18,26},{... | collective-permute-start | bytes 3145736 | tf_op jit(solution)/shard_map/ppermute | solution.py:115
  619.1 43.3 %collective-permute-start.64 = (bf16[512,1024]{1,0:T(8,128)(2,1)S(1)}, bf16[512,1024]{1,0:T(8,128)(2,1)S(1)}, u32[]{:S(2)}, u32[]{:S(2)}) collective-permute-start(bf16[512,1024]{1,0:T(8,128)(2,1)S(1)} %copy-done.30), channel_id=1, source_target_pairs={{8,0},{16,8},{24,16},{9,1},{17,9},{25,17},{10,2},{18,10},{26,18},{... | collective-permute-start | bytes 3145736 | tf_op jit(solution)/shard_map/ppermute | solution.py:116
  620.4 111.8 %collective-permute-start.30 = (bf16[256,2048]{1,0:T(8,128)(2,1)S(1)}, bf16[256,2048]{1,0:T(8,128)(2,1)}, u32[]{:S(2)}, u32[]{:S(2)}) collective-permute-start(bf16[256,2048]{1,0:T(8,128)(2,1)S(1)} %pad_maximum_fusion.3), channel_id=1, source_target_pairs={{0,4},{4,0},{1,5},{5,1},{2,6},{6,2},{3,7},{7,3},{8,12},{12,8},{9,1... | collective-permute-start | bytes 3145736 | tf_op jit(solution)/shard_map/ppermute | solution.py:29
  624.5 107.7 %collective-permute-start.28 = (bf16[256,2048]{1,0:T(8,128)(2,1)}, bf16[256,2048]{1,0:T(8,128)(2,1)}, u32[]{:S(2)}, u32[]{:S(2)}) collective-permute-start(bf16[256,2048]{1,0:T(8,128)(2,1)} %pad_maximum_fusion.2), channel_id=1, source_target_pairs={{0,1},{1,0},{2,3},{3,2},{4,5},{5,4},{6,7},{7,6},{8,9},{9,8},{10,11... | collective-permute-start | bytes 3145736 | tf_op jit(solution)/shard_map/ppermute | solution.py:29
  631.9 51.4 %collective-permute-start.35 = (bf16[256,2048]{1,0:T(8,128)(2,1)}, bf16[256,2048]{1,0:T(8,128)(2,1)}, u32[]{:S(2)}, u32[]{:S(2)}) collective-permute-start(bf16[256,2048]{1,0:T(8,128)(2,1)} %pad_maximum_fusion.5), channel_id=1, source_target_pairs={{0,4},{4,0},{1,5},{5,1},{2,6},{6,2},{3,7},{7,3},{8,12},{12,8},{9,1... | collective-permute-start | bytes 3145736 | tf_op jit(solution)/shard_map/ppermute | solution.py:29
  (113 other events, 1674.7 us)
Sparse Core Ops, SparseCore 0:
  50.6 25.2 all-gather.6
  78.0 62.9 all-gather.4
  143.2 98.7 all-gather.8
  244.0 83.8 all-gather.10

commit v2 on v1

v2 whole, which is shorter than its diff:
```python
import functools
import math

import jax
import jax.numpy as jnp
import numpy as np
from jax import lax
from jax.experimental import pallas as pl
from jax.experimental.pallas import tpu as pltpu
from jax.sharding import Mesh
from jax.sharding import PartitionSpec as P

HEAD = 64
ROT = 32
PAIR = 2 * HEAD
SCALE = HEAD ** (-0.5)

EPS_NORM = 1e-05
MASK_FILL = -1e30
BETA_ONE = 0.9
BETA_TWO = 0.95
ADAM_EPS = 1e-08
RATE = 0.02
DECAY = 0.1
STEP_COUNT = 10
GELU_ROOT = math.sqrt(2.0 / math.pi)
GELU_CUBE = 0.044715

BF16 = jnp.bfloat16
F32 = jnp.float32


def swap(value, axis):
    return lax.ppermute(value, axis, [(0, 1), (1, 0)])


def swap_inner(value, flip):
    return lax.ppermute(value, ("w", "c"), [(i, i ^ flip) for i in range(4)])


def ring(value):
    n = lax.axis_size("h")
    return lax.ppermute(value, "h", [(i, (i + 1) % n) for i in range(n)])


def inner_index():
    return 2 * lax.axis_index("w") + lax.axis_index("c")


def dp_index():
    outer = 2 * lax.axis_index("h") + lax.axis_index("w")
    return 4 * outer + 2 * lax.axis_index("y") + lax.axis_index("c")


def feature_table():
    n = lax.axis_size("h")
    h, w, y, c = (lax.axis_index(axis) for axis in "hwyc")
    entries = [lax.axis_index("t")]
    for flip_y in range(2):
        for back in range(n):
            for flip in range(4):
                outer = 2 * lax.rem(h + n - back, n) + (w ^ (flip >> 1))
                entries.append(4 * outer + 2 * (y ^ flip_y) + (c ^ (flip & 1)))
    return jnp.stack(entries).astype(jnp.int32)


def column_block(weight, j):
    width = weight.shape[-1] // 4
    return lax.dynamic_slice_in_dim(weight, j * width, width, weight.ndim - 1)


def attention_block(qkv_weight, out_weight, j):
    qkv = column_block(qkv_weight, j)
    return jnp.concatenate([qkv[0], qkv[1], qkv[2], column_block(out_weight, j)], axis=1)


def spread(piece_of):
    r = inner_index()
    pieces = [swap_inner(piece_of(r ^ flip), flip) for flip in range(1, 4)]
    return jnp.concatenate([piece_of(r), *pieces])


def collect(total):
    r = inner_index()
    rows = total.shape[0] // 4
    pieces = [(r, total[:rows])]
    for flip in range(1, 4):
        pieces.append((r ^ flip, swap_inner(total[flip * rows : (flip + 1) * rows], flip)))
    return pieces


def join_columns(pieces):
    rows, width = pieces[0][1].shape
    out = jnp.zeros((rows, 4 * width), BF16)
    for j, piece in pieces:
        out = lax.dynamic_update_slice(out, piece, (0, j * width))
    return out.astype(F32)


def join_attention(pieces):
    rows, width = pieces[0][1].shape[0], pieces[0][1].shape[1] // 4
    parts = []
    for i in range(4):
        parts.append(join_columns([(j, piece[:, i * width : (i + 1) * width]) for j, piece in pieces]))
    return jnp.stack(parts[:3]), parts[3]


class Gather:
    def __init__(self, own):
        self.beside = [own]
        self.far = []

    def over_h(self):
        for _ in range(lax.axis_size("h") - 1):
            self.beside.append(ring(self.beside[-1]))

    def over_y_first(self):
        self.far.append(swap(self.beside[0], "y"))

    def over_y_rest(self):
        self.far += [swap(piece, "y") for piece in self.beside[1:]]

    def pieces(self):
        return self.beside + self.far


class Reduce:
    def __init__(self, parts):
        n = len(parts) // 2
        self.own, self.beside, self.own_far, self.far = parts[0], parts[1:n], parts[n], parts[n + 1 :]

    def over_y_rest(self):
        self.beside = [near + swap(far, "y") for near, far in zip(self.beside, self.far)]
        self.far = []

    def over_h(self):
        moving = None
        for near in self.beside:
            moving = ring(near if moving is None else near + moving)
        self.beside = [] if moving is None else [moving]

    def over_y_first(self):
        self.own_far = swap(self.own_far, "y")

    def total(self):
        total = self.own.astype(F32) + self.own_far.astype(F32)
        return sum((near.astype(F32) for near in self.beside), total).astype(BF16)


class GroupSum:
    def __init__(self, parts):
        self.mine, self.other = parts

    def over_c(self):
        self.other = swap(self.other, "c")

    def block(self, sequence, half):
        rows = self.mine.shape[0] // 4
        start = ((2 * sequence + half) * rows, 0)
        size = (rows, self.mine.shape[1])
        return lax.dynamic_slice(self.mine, start, size) + lax.dynamic_slice(self.other, start, size)

    def corner(self):
        self.moving = swap(self.block(1, 1 - lax.axis_index("t")), "t")

    def edges(self):
        t = lax.axis_index("t")
        self.turning = swap(self.block(1, t) + self.moving, "w")
        self.moving = swap(self.block(0, 1 - t), "t")

    def total(self):
        own = self.block(0, lax.axis_index("t"))
        return own.astype(F32) + self.moving.astype(F32) + self.turning.astype(F32)


def close(*items):
    holders = [vars(item) if isinstance(item, (Gather, Reduce, GroupSum)) else item for item in items]
    held = lax.optimization_barrier(holders)
    out = []
    for item, value in zip(items, held):
        if isinstance(item, (Gather, Reduce, GroupSum)):
            vars(item).update(value)
        else:
            out.append(value)
    return out


def flips_outer(value):
    n = lax.axis_size("h")
    bit = 1
    while bit < n:
        value = value + lax.ppermute(value, "h", [(i, i ^ bit) for i in range(n)])
        bit *= 2
    return value


def gather_vectors(pair):
    count = 8 * lax.axis_size("h")
    out = jnp.zeros((2, count * pair.shape[1]), pair.dtype)
    out = lax.dynamic_update_slice(out, pair, (0, dp_index() * pair.shape[1]))
    for axis in "wyc":
        out = out + swap(out, axis)
    return flips_outer(out)


def sum_vectors(pair):
    for axis in "ctyw":
        pair = pair + swap(pair, axis)
    pair = flips_outer(pair)
    width = pair.shape[1] // (8 * lax.axis_size("h"))
    return lax.dynamic_slice(pair, (0, dp_index() * width), (2, width))


def lane_tables(length):
    position = np.arange(length, dtype=np.float32)[:, None]
    inverse = 10000.0 ** (-(np.arange(ROT // 2, dtype=np.float32) * 2.0 / ROT))
    angles = (position * inverse.astype(np.float32)[None, :]).astype(np.float64)
    cosine = jnp.asarray(np.cos(angles).astype(np.float32))
    sine = jnp.asarray(np.sin(angles).astype(np.float32))
    none = jnp.zeros_like(sine)
    rest = jnp.zeros((length, HEAD - ROT), F32)
    tables = (
        jnp.concatenate([cosine, cosine, rest + 1.0], axis=1),
        jnp.concatenate([sine, none, rest], axis=1),
        jnp.concatenate([none, sine, rest], axis=1),
    )
    return tuple(jnp.concatenate([table, table], axis=1) for table in tables)


def attention_body(proj_ref, grad_ref, cos_ref, low_ref, high_ref, context_ref, d_proj_ref):
    length, width = grad_ref.shape
    half = length // 2
    cosine, low, high = cos_ref[...], low_ref[...], high_ref[...]
    first = lax.broadcasted_iota(jnp.int32, (length, PAIR), 1) < HEAD
    row = lax.broadcasted_iota(jnp.int32, (half, half), 0)
    col = lax.broadcasted_iota(jnp.int32, (half, half), 1)
    keep = row <= col

    def turn(value, sign):
        ahead = pltpu.roll(value, PAIR - ROT // 2, 1)
        behind = pltpu.roll(value, ROT // 2, 1)
        return value * cosine - sign * ahead * low + sign * behind * high

    def rows_by_rows(a, b):
        return lax.dot_general(a, b, (((1,), (1,)), ((), ())), preferred_element_type=F32)

    def turned(a, b):
        return lax.dot_general(a, b, (((0,), (0,)), ((), ())), preferred_element_type=F32)

    def plain(a, b):
        return lax.dot_general(a, b, (((1,), (0,)), ((), ())), preferred_element_type=F32)

    def over_keys(function, value):
        return function(value, axis=0, keepdims=True)

    for pair in range(width // PAIR):
        lanes = pl.ds(pair * PAIR, PAIR)
        key_lanes = pl.ds(width + pair * PAIR, PAIR)
        value_lanes = pl.ds(2 * width + pair * PAIR, PAIR)
        query = (turn(proj_ref[:, lanes], 1.0).astype(BF16).astype(F32) * SCALE).astype(BF16)
        keys = turn(proj_ref[:, key_lanes], 1.0).astype(BF16)
        values = proj_ref[:, value_lanes].astype(BF16)
        grad = grad_ref[:, lanes]
        context = jnp.zeros((length, PAIR), F32)
        d_query = context
        d_keys_a = d_keys_b = d_values_a = d_values_b = jnp.zeros((half, PAIR), F32)
        for head in range(2):
            mine = first if head == 0 else jnp.logical_not(first)
            q, k, v, g = (
                jnp.where(mine, item, jnp.zeros_like(item)) for item in (query, keys, values, grad)
            )
            qa, qb, ga, gb = q[:half], q[half:], g[:half], g[half:]
            s_aa = jnp.where(keep, rows_by_rows(keys[:half], qa), MASK_FILL)
            s_ab = rows_by_rows(keys[:half], qb)
            s_bb = jnp.where(keep, rows_by_rows(keys[half:], qb), MASK_FILL)
            max_a = over_keys(jnp.max, s_aa)
            max_b = jnp.maximum(over_keys(jnp.max, s_ab), over_keys(jnp.max, s_bb))
            e_aa, e_ab, e_bb = jnp.exp(s_aa - max_a), jnp.exp(s_ab - max_b), jnp.exp(s_bb - max_b)
            inv_a = 1.0 / over_keys(jnp.sum, e_aa)
            inv_b = 1.0 / (over_keys(jnp.sum, e_ab) + over_keys(jnp.sum, e_bb))
            p_aa, p_ab, p_bb = e_aa * inv_a, e_ab * inv_b, e_bb * inv_b
            r_aa, r_ab, r_bb = p_aa.astype(BF16), p_ab.astype(BF16), p_bb.astype(BF16)
            d_aa = rows_by_rows(values[:half], ga)
            d_ab = rows_by_rows(values[:half], gb)
            d_bb = rows_by_rows(values[half:], gb)
            centre_a = over_keys(jnp.sum, d_aa * p_aa)
            centre_b = over_keys(jnp.sum, d_ab * p_ab) + over_keys(jnp.sum, d_bb * p_bb)
            t_aa = (p_aa * (d_aa - centre_a)).astype(BF16)
            t_ab = (p_ab * (d_ab - centre_b)).astype(BF16)
            t_bb = (p_bb * (d_bb - centre_b)).astype(BF16)
            context += jnp.concatenate(
                [turned(r_aa, v[:half]), turned(r_ab, v[:half]) + turned(r_bb, v[half:])]
            )
            d_query += jnp.concatenate(
                [turned(t_aa, k[:half]), turned(t_ab, k[:half]) + turned(t_bb, k[half:])]
            )
            d_keys_a += plain(t_aa, qa) + plain(t_ab, qb)
            d_keys_b += plain(t_bb, qb)
            d_values_a += plain(r_aa, ga) + plain(r_ab, gb)
            d_values_b += plain(r_bb, gb)
        context_ref[:, lanes] = context.astype(BF16)
        d_proj_ref[:, lanes] = turn(d_query * SCALE, -1.0).astype(BF16)
        d_keys = jnp.concatenate([d_keys_a, d_keys_b])
        d_proj_ref[:, key_lanes] = turn(d_keys, -1.0).astype(BF16)
        d_proj_ref[:, value_lanes] = jnp.concatenate([d_values_a, d_values_b]).astype(BF16)


def dot_nn(a, b):
    return lax.dot_general(a, b, (((1,), (0,)), ((), ())), preferred_element_type=F32)


def dot_nt(a, b):
    return lax.dot_general(a, b, (((1,), (1,)), ((), ())), preferred_element_type=F32)


def dot_tn(a, b):
    return lax.dot_general(a, b, (((0,), (0,)), ((), ())), preferred_element_type=F32)


def rows_of(block, width):
    return pl.BlockSpec((block, width), lambda s: (s, 0))


def whole(shape):
    return pl.BlockSpec(shape, lambda s: (0, 0), pipeline_mode=pl.Buffered(1))


ANYWHERE = pl.BlockSpec(memory_space=pl.ANY)
PARAMS = pltpu.CompilerParams(vmem_limit_bytes=58 << 20)


def fetch(piece_refs, into_ref, sem_ref, start=0):
    width = into_ref.shape[1]

    @pl.when(pl.program_id(0) == 0)
    def _():
        copies = []
        for i, piece in enumerate(piece_refs):
            rows = piece.shape[0]
            copies.append(
                pltpu.make_async_copy(
                    piece.at[:, pl.ds(start, width)],
                    into_ref.at[pl.ds(i * rows, rows), :],
                    sem_ref.at[i],
                )
            )
        for copy in copies:
            copy.start()
        for copy in copies:
            copy.wait()


def join_step(table_ref, *refs, norm, permute):
    pieces, (gain_ref, bias_ref, out_ref, buffer, sems) = refs[:8], refs[8:]
    step = pl.program_id(0)
    features = out_ref.shape[1]
    blocks = table_ref.shape[0] - 1 if permute else 1
    size = features // blocks

    def copy(i, slot):
        return pltpu.make_async_copy(pieces[i], buffer.at[slot], sems.at[slot])

    for i in range(8):
        pl.when(step == max(i - 1, 0))(lambda i=i: copy(i, i % 2).start())
    slot = lax.rem(step, 2)
    copy(0, slot).wait()
    chunk = min(128, out_ref.shape[0])

    def emit(i, carry):
        at = pl.ds(pl.multiple_of(i * chunk, chunk), chunk)
        if norm:
            rows = buffer[slot, at, :].astype(F32)
            mean = jnp.mean(rows, axis=1, keepdims=True)
            centred = rows - mean
            inv_std = lax.rsqrt(jnp.mean(centred * centred, axis=1, keepdims=True) + EPS_NORM)
        for j in range(blocks):
            lanes = pl.ds(pl.multiple_of(table_ref[1 + j] * size, size), size) if permute else slice(None)
            value = buffer[slot, at, lanes]
            if norm:
                normed = (value.astype(F32) - mean) * inv_std
                value = (normed * gain_ref[:, lanes] + bias_ref[:, lanes]).astype(BF16)
            out_ref[at, j * size : (j + 1) * size] = value
        return carry

    lax.fori_loop(0, out_ref.shape[0] // chunk, emit, 0)


def join(table, pieces, gain, bias, norm):
    block, features = pieces[0].shape
    blocks = table.shape[0] - 1
    permute = features // blocks % 128 == 0
    vector = pl.BlockSpec((1, features), lambda s, h: (0, 0))
    out = pl.pallas_call(
        functools.partial(join_step, norm=norm, permute=permute),
        grid_spec=pltpu.PrefetchScalarGridSpec(
            num_scalar_prefetch=1,
            grid=(8,),
            in_specs=[ANYWHERE] * 8 + [vector, vector],
            out_specs=pl.BlockSpec((block, features), lambda s, h: (s - s % 2 + (s + h[0]) % 2, 0)),
            scratch_shapes=[
                pltpu.VMEM((2, block, features), BF16),
                pltpu.SemaphoreType.DMA((2,)),
            ],
        ),
        out_shape=jax.ShapeDtypeStruct((8 * block, features), BF16),
        compiler_params=PARAMS,
        name="join",
    )(table, *pieces, gain, bias)
    if not permute:
        cut = out.reshape(8 * block, blocks, features // blocks)
        out = jnp.take(cut, table[1:], axis=1).reshape(8 * block, features)
    return out


def add_and_flush(total_ref, part_refs, addends):
    step = pl.program_id(0)

    @pl.when(step == 0)
    def _():
        total_ref[...] = jnp.zeros_like(total_ref)

    for lanes, addend in addends:
        total_ref[:, lanes] += addend()

    @pl.when(step == pl.num_programs(0) - 1)
    def _():
        rows = part_refs[0].shape[0]
        for i, part_ref in enumerate(part_refs):
            part_ref[...] = total_ref[i * rows : (i + 1) * rows, :].astype(BF16)


def attention_step(hidden_ref, cotan_ref, cos_ref, low_ref, high_ref, *refs):
    pieces, (context_ref, d_proj_ref, cols_ref, proj_ref, grad_ref, sems) = refs[:-6], refs[-6:]
    fetch(pieces, cols_ref, sems)
    width = grad_ref.shape[1]
    proj_ref[...] = dot_nn(hidden_ref[...], cols_ref[:, : 3 * width])
    grad_ref[...] = dot_nn(cotan_ref[...], cols_ref[:, 3 * width :]).astype(BF16)
    attention_body(proj_ref, grad_ref, cos_ref, low_ref, high_ref, context_ref, d_proj_ref)


def attention(hidden, cotan, pieces, length):
    tokens, features = hidden.shape
    width = pieces[0].shape[1] // 4
    return pl.pallas_call(
        attention_step,
        grid=(tokens // length,),
        in_specs=[rows_of(length, features)] * 2
        + [whole((length, PAIR))] * 3
        + [ANYWHERE] * len(pieces),
        out_specs=(rows_of(length, width), rows_of(length, 3 * width)),
        out_shape=(
            jax.ShapeDtypeStruct((tokens, width), BF16),
            jax.ShapeDtypeStruct((tokens, 3 * width), BF16),
        ),
        scratch_shapes=[
            pltpu.VMEM((features, 4 * width), BF16),
            pltpu.VMEM((length, 3 * width), F32),
            pltpu.VMEM((length, width), BF16),
            pltpu.SemaphoreType.DMA((len(pieces),)),
        ],
        compiler_params=PARAMS,
        name="attention",
    )(hidden, cotan, *lane_tables(length), *pieces)


def parts_of(count, features, width):
    rows = features // count
    shapes = [jax.ShapeDtypeStruct((rows, width), BF16)] * count
    return [whole((rows, width))] * count, shapes, [pltpu.VMEM((features, width), F32)]


def attention_grads_step(hidden_ref, cotan_ref, d_proj_ref, context_ref, *refs):
    wide = d_proj_ref.shape[1]
    add_and_flush(
        refs[-1],
        refs[:-1],
        [
            (pl.ds(0, wide), lambda: dot_tn(hidden_ref[...], d_proj_ref[...])),
            (pl.ds(wide, wide // 3), lambda: dot_tn(cotan_ref[...], context_ref[...])),
        ],
    )


def attention_grads(hidden, cotan, d_proj, context, block, count):
    tokens, features = hidden.shape
    width = context.shape[1]
    specs, shapes, scratch = parts_of(count, features, 4 * width)
    return pl.pallas_call(
        attention_grads_step,
        grid=(tokens // block,),
        in_specs=[rows_of(block, features)] * 2 + [rows_of(block, 3 * width), rows_of(block, width)],
        out_specs=specs,
        out_shape=shapes,
        scratch_shapes=scratch,
        compiler_params=PARAMS,
        name="attention_grads",
    )(hidden, cotan, d_proj, context)


def fc1_step(hidden_ref, cotan_ref, *refs, count):
    pieces, (act_ref, slope_ref), parts = refs[:count], refs[count : count + 2], refs[count + 2 : -3]
    cols_ref, total_ref, sems = refs[-3:]
    fetch(pieces, cols_ref, sems)
    pre = dot_nn(hidden_ref[...], cols_ref[...])
    square = pre * pre
    tanh = jnp.tanh(GELU_ROOT * (pre + GELU_CUBE * (pre * square)))
    half = 0.5 * (1.0 + tanh)
    slope = 0.5 * GELU_ROOT * pre * (1.0 - tanh * tanh) * (1.0 + 3.0 * GELU_CUBE * square)
    act_ref[...] = (pre * half).astype(BF16)
    slope_ref[...] = half + slope
    every = pl.ds(0, total_ref.shape[1])
    add_and_flush(total_ref, parts, [(every, lambda: dot_tn(cotan_ref[...], act_ref[...]))])


def fc1_pass(hidden, cotan, pieces, block):
    tokens, features = hidden.shape
    count, width = len(pieces), pieces[0].shape[1]
    specs, shapes, scratch = parts_of(count, features, width)
    act, slope, *parts = pl.pallas_call(
        functools.partial(fc1_step, count=count),
        grid=(tokens // block,),
        in_specs=[rows_of(block, features)] * 2 + [ANYWHERE] * count,
        out_specs=[rows_of(block, width)] * 2 + specs,
        out_shape=[
            jax.ShapeDtypeStruct((tokens, width), BF16),
            jax.ShapeDtypeStruct((tokens, width), F32),
            *shapes,
        ],
        scratch_shapes=[
            pltpu.VMEM((features, width), BF16),
            *scratch,
            pltpu.SemaphoreType.DMA((count,)),
        ],
        compiler_params=PARAMS,
        name="fc1_pass",
    )(hidden, cotan, *pieces)
    return act, slope, parts


def fc2_step(hidden_ref, cotan_ref, slope_ref, *refs, count):
    pieces, d_pre_ref, parts = refs[:count], refs[count], refs[count + 1 : -3]
    cols_ref, total_ref, sems = refs[-3:]
    fetch(pieces, cols_ref, sems)
    d_pre_ref[...] = (dot_nn(cotan_ref[...], cols_ref[...]) * slope_ref[...]).astype(BF16)
    every = pl.ds(0, total_ref.shape[1])
    add_and_flush(total_ref, parts, [(every, lambda: dot_tn(hidden_ref[...], d_pre_ref[...]))])


def fc2_pass(hidden, cotan, pieces, slope, block):
    tokens, features = hidden.shape
    count, width = len(pieces), pieces[0].shape[1]
    specs, shapes, scratch = parts_of(count, features, width)
    d_pre, *parts = pl.pallas_call(
        functools.partial(fc2_step, count=count),
        grid=(tokens // block,),
        in_specs=[rows_of(block, features)] * 2 + [rows_of(block, width)] + [ANYWHERE] * count,
        out_specs=[rows_of(block, width)] + specs,
        out_shape=[jax.ShapeDtypeStruct((tokens, width), BF16), *shapes],
        scratch_shapes=[
            pltpu.VMEM((features, width), BF16),
            *scratch,
            pltpu.SemaphoreType.DMA((count,)),
        ],
        compiler_params=PARAMS,
        name="fc2_pass",
    )(hidden, cotan, slope, *pieces)
    return d_pre, parts


def back_step(table_ref, first_ref, second_ref, *refs, count, start, permute):
    attn_pieces, fc_pieces, (mine_ref, other_ref) = refs[:count], refs[count:-6], refs[-6:-4]
    attn_ref, fc_ref, attn_sems, fc_sems = refs[-4:]
    fetch(attn_pieces, attn_ref, attn_sems, start)
    fetch(fc_pieces, fc_ref, fc_sems)
    out = dot_nt(first_ref[...], attn_ref[...]) + dot_nt(second_ref[...], fc_ref[...])
    out = out.astype(BF16)
    middle = pl.num_programs(0) // 2
    blocks = table_ref.shape[0] - 1
    size = out.shape[1] // blocks

    def store(out_ref):
        if not permute:
            out_ref[...] = out
            return
        for j in range(blocks):
            lanes = pl.ds(pl.multiple_of(table_ref[1 + j] * size, size), size)
            out_ref[:, lanes] = out[:, j * size : (j + 1) * size]

    pl.when(pl.program_id(0) < middle)(lambda: store(mine_ref))
    pl.when(pl.program_id(0) >= middle)(lambda: store(other_ref))


def back_product(table, first, second, attn_pieces, fc_pieces, start, block):
    (tokens, size), width = first.shape, second.shape[1]
    count = len(attn_pieces)
    features = count * attn_pieces[0].shape[0]
    blocks = table.shape[0] - 1
    permute = features // blocks % 128 == 0
    middle = tokens // block // 2
    outs = pl.pallas_call(
        functools.partial(back_step, count=count, start=start, permute=permute),
        grid_spec=pltpu.PrefetchScalarGridSpec(
            num_scalar_prefetch=1,
            grid=(tokens // block,),
            in_specs=[
                pl.BlockSpec((block, size), lambda s, h: (s, 0)),
                pl.BlockSpec((block, width), lambda s, h: (s, 0)),
            ]
            + [ANYWHERE] * (2 * count),
            out_specs=(
                pl.BlockSpec((block, features), lambda s, h: (jnp.minimum(s, middle - 1), 0)),
                pl.BlockSpec((block, features), lambda s, h: (jnp.maximum(s - middle, 0), 0)),
            ),
            scratch_shapes=[
                pltpu.VMEM((features, size), BF16),
                pltpu.VMEM((features, width), BF16),
                pltpu.SemaphoreType.DMA((count,)),
                pltpu.SemaphoreType.DMA((count,)),
            ],
        ),
        out_shape=(jax.ShapeDtypeStruct((tokens // 2, features), BF16),) * 2,
        compiler_params=PARAMS,
        name="back_product",
    )(table, first, second, *attn_pieces, *fc_pieces)
    if not permute:
        order = jnp.argsort(table[1:])
        cut = [out.reshape(tokens // 2, blocks, features // blocks) for out in outs]
        outs = [jnp.take(out, order, axis=1).reshape(tokens // 2, features) for out in cut]
    return outs


def adamw(weight, gradient, moment, second):
    new_m = BETA_ONE * moment + (1.0 - BETA_ONE) * gradient
    new_v = BETA_TWO * second + (1.0 - BETA_TWO) * gradient * gradient
    m_hat = new_m / (1.0 - BETA_ONE**STEP_COUNT)
    v_hat = new_v / (1.0 - BETA_TWO**STEP_COUNT)
    update = -RATE * (m_hat / (jnp.sqrt(v_hat) + ADAM_EPS) + DECAY * weight.astype(F32))
    return (gradient, update, new_m, new_v)


def shards(
    inputs,
    ln_gain,
    ln_bias,
    qkv_weight,
    out_weight,
    fc1_weight,
    fc2_weight,
    cotangent,
    m_gain,
    v_gain,
    m_bias,
    v_bias,
    m_qkv,
    v_qkv,
    m_out,
    v_out,
    m_fc1,
    v_fc1,
    m_fc2,
    v_fc2,
):
    length = 2 * inputs.shape[0]
    block = length // 2
    count = 2 * lax.axis_size("h")
    table = feature_table()

    attn = Gather(spread(functools.partial(attention_block, qkv_weight, out_weight)))
    x, g = [inputs, swap(inputs, "t"), swap(inputs, "w")], [cotangent]
    x_other, g_other = [swap(inputs, "c")], [swap(cotangent, "c")]
    vectors = gather_vectors(jnp.stack([ln_gain, ln_bias]))
    x, g, x_other, g_other, vectors, fc1_late, fc2_late = close(attn, x, g, x_other, g_other, vectors, fc1_weight, fc2_weight)
    attn.over_h()
    attn.over_y_first()
    g += [swap(g[0], "t"), swap(g[0], "w")]
    x.append(swap(x[2], "t"))
    x_other += [swap(x[1], "c"), swap(x[2], "c"), swap(x[3], "c")]
    fc1 = Gather(spread(functools.partial(column_block, fc1_late)))
    x, g, x_other, g_other, vectors, fc2_late = close(attn, fc1, x, g, x_other, g_other, vectors, fc2_late)
    fc1.over_h()
    fc1.over_y_first()
    attn.over_y_rest()
    g.append(swap(g[2], "t"))
    g_other += [swap(g[1], "c"), swap(g[2], "c"), swap(g[3], "c")]
    gain_wide, bias_wide = vectors[:1].astype(F32), vectors[1:].astype(F32)
    fc2 = Gather(spread(functools.partial(column_block, fc2_late)))
    hidden = join(table, x + x_other, gain_wide, bias_wide, True)
    g, g_other, hidden = close(fc1, attn, fc2, g, g_other, hidden)
    fc2.over_h()
    fc2.over_y_first()
    fc1.over_y_rest()
    cotan = join(table, g + g_other, gain_wide, bias_wide, False)
    context, d_proj = attention(hidden, cotan, attn.pieces(), length)
    attn_parts = attention_grads(hidden, cotan, d_proj, context, block, count)
    hidden, cotan, context, d_proj, attn_parts = close(attn, fc1, fc2, hidden, cotan, context, d_proj, attn_parts)
    fc2.over_y_rest()
    attn_sum = Reduce(attn_parts)
    attn_sum.over_y_rest()
    act, slope, fc2_parts = fc1_pass(hidden, cotan, fc1.pieces(), block)
    hidden, cotan, context, d_proj, act, slope, fc2_parts = close(attn, fc1, fc2, attn_sum, hidden, cotan, context, d_proj, act, slope, fc2_parts)
    attn_sum.over_h()
    attn_sum.over_y_first()
    fc2_sum = Reduce(fc2_parts)
    fc2_sum.over_y_rest()
    start = d_proj.shape[1]
    d_pre, fc1_parts = fc2_pass(hidden, cotan, fc2.pieces(), slope, block)
    d_hidden = GroupSum(back_product(table, d_proj, d_pre, attn.pieces(), fc1.pieces(), 0, block))
    context, act, fc1_parts = close(attn, fc2, attn_sum, fc2_sum, d_hidden, context, act, fc1_parts)
    fc2_sum.over_h()
    fc2_sum.over_y_first()
    fc1_sum = Reduce(fc1_parts)
    fc1_sum.over_y_rest()
    d_hidden.over_c()
    d_hidden.corner()
    branch = GroupSum(back_product(table, context, act, attn.pieces(), fc2.pieces(), start, block))
    attn_pieces = collect(attn_sum.total())
    (attn_pieces,) = close(fc1_sum, fc2_sum, d_hidden, branch, attn_pieces)
    fc1_sum.over_h()
    fc1_sum.over_y_first()
    d_hidden.edges()
    branch.over_c()
    branch.corner()
    qkv_grad, out_grad = join_attention(attn_pieces)
    qkv_res = adamw(qkv_weight, qkv_grad, m_qkv, v_qkv)
    out_res = adamw(out_weight, out_grad, m_out, v_out)
    fc2_pieces = collect(fc2_sum.total())
    (fc2_pieces,) = close(fc1_sum, d_hidden, branch, fc2_pieces)
    branch.edges()
    fc1_res = adamw(fc1_weight, join_columns(collect(fc1_sum.total())), m_fc1, v_fc1)
    fc2_res = adamw(fc2_weight, join_columns(fc2_pieces), m_fc2, v_fc2)
    d_hidden = d_hidden.total()
    own_rows = inputs.astype(F32)
    output = (own_rows + branch.total()).astype(BF16)

    centred = own_rows - jnp.mean(own_rows, axis=1, keepdims=True)
    inv_std = lax.rsqrt(jnp.mean(centred * centred, axis=1, keepdims=True) + EPS_NORM)
    normed = centred * inv_std
    vector_parts = jnp.stack([jnp.sum(d_hidden * normed, axis=0), jnp.sum(d_hidden, axis=0)])
    vector_grads = sum_vectors(vector_parts)
    scaled_grad = d_hidden * vectors[:1].astype(F32)
    input_grad = cotangent.astype(F32) + inv_std * (
        scaled_grad
        - jnp.mean(scaled_grad, axis=1, keepdims=True)
        - normed * jnp.mean(scaled_grad * normed, axis=1, keepdims=True)
    )
    gain_res = adamw(ln_gain, vector_grads[0], m_gain, v_gain)
    bias_res = adamw(ln_bias, vector_grads[1], m_bias, v_bias)
    return (
        output,
        input_grad,
        *gain_res,
        *bias_res,
        *qkv_res,
        *out_res,
        *fc1_res,
        *fc2_res,
    )


def solution(mesh):
    dp, tensor = mesh.devices.shape
    inner = Mesh(mesh.devices.reshape(dp // 8, 2, 2, 2, tensor), ("h", "w", "y", "c", "t"))
    rows = P(("h", "w", "y", "c", "t"), None)
    vector = P(("h", "w", "y", "c"))
    stack = P(None, ("h", "w", "y", "c"), "t")
    matrix = P(("h", "w", "y", "c"), "t")
    return jax.shard_map(
        shards,
        mesh=inner,
        in_specs=(rows, vector, vector, stack, matrix, matrix, matrix, rows)
        + (vector,) * 4
        + (stack,) * 2
        + (matrix,) * 6,
        out_specs=(rows, rows) + (vector,) * 8 + (stack,) * 4 + (matrix,) * 12,
        check_vma=False,
    )
```

time: 752 us -> 566 us (0.75)
  Pallas kernels: 17.1 us -> 181 us
  matrix products: 146 us -> 0 us
  starting transfers between devices: 165 us -> 64.5 us
  waiting for transfers between devices: 277 us -> 237 us
  local copies, waits for them, and re-layouts: 52.2 us -> 26.4 us
  other arithmetic: 71.6 us -> 50.5 us
  between operations: 15.6 us -> 2.05 us
    pallas_call x1 -> x8, Pallas kernels: 17.1 us -> 181 us  [the longest x2 49 us: back_product(): pl.pallas_call(functools.partial(back_step, count=count, start=start, per...]
    dot_general x12 -> x0, matrix products: 146 us -> none  [the longest x4 54.7 us: dot_nt(): lax.dot_general(a, b, (((1,), (1,)), ((), ())), preferred_element_type=F32)]
    ppermute x52 -> x26, starting transfers between devices: 142 us -> 29.4 us  [the longest x18 16.8 us: swap_inner(): return lax.ppermute(value, ('w', 'c'), [(i, i ^ flip) for i in range(4)])]
    all_gather x4 -> x0, waiting for transfers between devices: 75.1 us -> none  [gather_outer(): return lax.all_gather(value, 'o', axis=0, tiled=True)]
    ppermute x25 -> x41, waiting for transfers between devices: 71.6 us -> 89.7 us  [swap(): return lax.ppermute(value, axis, [(0, 1), (1, 0)])]
    ppermute x52 -> x26, waiting for transfers between devices: 130 us -> 147 us  [the longest x18 99 us: swap_inner(): return lax.ppermute(value, ('w', 'c'), [(i, i ^ flip) for i in range(4)])]
    ppermute x25 -> x41, starting transfers between devices: 23.1 us -> 35.1 us  [swap(): return lax.ppermute(value, axis, [(0, 1), (1, 0)])]
    add x32 -> x16, other arithmetic: 28.7 us -> 17.1 us  [the longest x3 10 us: block(): lax.dynamic_slice(self.mine, start, size)]
  transfers between devices with their start and end apart: 81 -> 67, of which waited for: 33 -> 28; matrix products, arithmetic and copies ran while one was open for 34% -> 11% of each run, Pallas kernels for 2% -> 32%
where the time goes in v2:
time: 566 us; the launch traced here: 562 us
  waiting for transfers between devices  237 us (42%)
  Pallas kernels  181 us (32%)
  starting transfers between devices  64.5 us (11%)
  other arithmetic  50.5 us (9%)
  local copies, waits for them, and re-layouts  26.4 us (5%)
    ppermute x18, waiting for transfers between devices, swap_inner(): return lax.ppermute(value, ('w', 'c'), [(i, i ^ flip) for i in range(4)])  99 us
    ppermute x41, waiting for transfers between devices, swap(): return lax.ppermute(value, axis, [(0, 1), (1, 0)])  89.7 us
    pallas_call x2, Pallas kernels, back_product(): pl.pallas_call(functools.partial(back_step, count=count, start=start, per...  49 us
    ppermute x41, starting transfers between devices, swap(): return lax.ppermute(value, axis, [(0, 1), (1, 0)])  35.1 us
    pallas_call x1, Pallas kernels, fc1_pass(): pl.pallas_call(functools.partial(fc1_step, count=count), grid=(tokens //...  32.3 us
    ppermute x6, waiting for transfers between devices, ring(): return lax.ppermute(value, 'h', [(i, (i + 1) % n) for i in range(n)])  30.1 us
    pallas_call x1, Pallas kernels, attention(): pl.pallas_call(attention_step, grid=(tokens // length,), in_specs=[rows_o...  29.9 us
    pallas_call x1, Pallas kernels, fc2_pass(): pl.pallas_call(functools.partial(fc2_step, count=count), grid=(tokens //...  28.1 us
  transfers between devices with their start and end apart: 67, of which 28 were waited for; matrix products, arithmetic and copies ran while one was open for 11% of the time, Pallas kernels for 32%

profile of v2, /device:TPU:0, one launch (start us, length us, event | category | flops | bytes accessed | tf_op | source)
XLA Modules:
  0.0 561.7 jit_solution(1774077139721343836)
XLA Ops:
  15.3 13.4 %collective-permute-done.10 = bf16[2,2048]{1,0:T(2,128)(2,1)S(1)} collective-permute-done((bf16[2,2048]{1,0:T(2,128)(2,1)S(1)}, bf16[2,2048]{1,0:T(2,128)(2,1)S(1)}, u32[]{:S(2)}, u32[]{:S(2)}) %collective-permute-start.10) | collective-permute-done | bytes 8224 | tf_op jit(solution)/shard_map/ppermute | solution.py:192
  56.2 23.8 %collective-permute-done.15 = bf16[128,1024]{1,0:T(8,128)(2,1)S(1)} collective-permute-done((bf16[128,1024]{1,0:T(8,128)(2,1)S(1)}, bf16[128,1024]{1,0:T(8,128)(2,1)S(1)}, u32[]{:S(2)}, u32[]{:S(2)}) %collective-permute-start.15) | collective-permute-done | bytes 262176 | tf_op jit(solution)/shard_map/ppermute | solution.py:38
  87.8 9.9 %collective-permute-done.11.refs_1_ = bf16[512,1024]{1,0:T(8,128)(2,1)S(1)} collective-permute-done((bf16[512,1024]{1,0:T(8,128)(2,1)S(1)}, bf16[512,1024]{1,0:T(8,128)(2,1)S(1)}, u32[]{:S(2)}, u32[]{:S(2)}) %collective-permute-start.11) | collective-permute-done | bytes 1048608 | tf_op jit(solution)/shard_map/ppermute | solution.py:43
  98.8 10.4 %collective-permute-done.17.refs_1_ = bf16[256,2048]{1,0:T(8,128)(2,1)} collective-permute-done((bf16[256,2048]{1,0:T(8,128)(2,1)S(1)}, bf16[256,2048]{1,0:T(8,128)(2,1)}, u32[]{:S(2)}, u32[]{:S(2)}) %collective-permute-start.17) | collective-permute-done | bytes 1048608 | tf_op jit(solution)/shard_map/ppermute | solution.py:34
  109.2 10.9 %collective-permute-done.18.refs_2_ = bf16[256,2048]{1,0:T(8,128)(2,1)} collective-permute-done((bf16[256,2048]{1,0:T(8,128)(2,1)S(1)}, bf16[256,2048]{1,0:T(8,128)(2,1)}, u32[]{:S(2)}, u32[]{:S(2)}) %collective-permute-start.18) | collective-permute-done | bytes 1048608 | tf_op jit(solution)/shard_map/ppermute | solution.py:34
  124.3 25.8 %collective-permute-done.27 = bf16[128,1024]{1,0:T(8,128)(2,1)S(1)} collective-permute-done((bf16[128,1024]{1,0:T(8,128)(2,1)S(1)}, bf16[128,1024]{1,0:T(8,128)(2,1)S(1)}, u32[]{:S(2)}, u32[]{:S(2)}) %collective-permute-start.27) | collective-permute-done | bytes 262176 | tf_op jit(solution)/shard_map/ppermute | solution.py:38
  156.4 12.3 %collective-permute-done.22.refs_1_.refs_5_ = bf16[512,1024]{1,0:T(8,128)(2,1)S(1)} collective-permute-done((bf16[512,1024]{1,0:T(8,128)(2,1)S(1)}, bf16[512,1024]{1,0:T(8,128)(2,1)S(1)}, u32[]{:S(2)}, u32[]{:S(2)}) %collective-permute-start.22) | collective-permute-done | bytes 1048608 | tf_op jit(solution)/shard_map/ppermute | solution.py:43
  170.6 14.6 %join.2.hidden_ref = bf16[2048,2048]{1,0:T(8,128)(2,1)} custom-call(s32[17]{0:T(128)} %stack.130.table_ref, bf16[256,2048]{1,0:T(8,128)(2,1)} %refs_0_, bf16[256,2048]{1,0:T(8,128)(2,1)} %copy-done.21, bf16[256,2048]{1,0:T(8,128)(2,1)} %copy-done.22, bf16[256,2048]{1,0:T(8,128)(2,1)} %collective-permute-done.16.refs_3_, ...), custom_call_target="tpu_custom_call" | custom-call | tf_op jit(solution)/shard_map/join/pallas_call | solution.py:393
  185.3 10.7 %collective-permute-done.24.refs_3_ = bf16[512,1024]{1,0:T(8,128)(2,1)} collective-permute-done((bf16[512,1024]{1,0:T(8,128)(2,1)S(1)}, bf16[512,1024]{1,0:T(8,128)(2,1)}, u32[]{:S(2)}, u32[]{:S(2)}) %collective-permute-start.24) | collective-permute-done | bytes 1048608 | tf_op jit(solution)/shard_map/ppermute | solution.py:34
  202.5 11.2 %join.3.cotan_ref = bf16[2048,2048]{1,0:T(8,128)(2,1)} custom-call(s32[17]{0:T(128)} %stack.130.table_ref, bf16[256,2048]{1,0:T(8,128)(2,1)} %refs_0_.1, bf16[256,2048]{1,0:T(8,128)(2,1)} %collective-permute-done.17.refs_1_, bf16[256,2048]{1,0:T(8,128)(2,1)} %collective-permute-done.18.refs_2_, bf16[256,2048]{1,0:T(8,128)(2,1)} %collective-permute-done.28.refs_3_, ...), custom_call_target="tpu_custom_call" | custom-call | tf_op jit(solution)/shard_map/join/pallas_call | solution.py:393
  213.7 29.9 %attention.1 = (bf16[2048,256]{1,0:T(8,128)(2,1)}, bf16[2048,768]{1,0:T(8,128)(2,1)}) custom-call(bf16[2048,2048]{1,0:T(8,128)(2,1)} %join.2.hidden_ref, bf16[2048,2048]{1,0:T(8,128)(2,1)} %join.3.cotan_ref, f32[512,128]{1,0:T(8,128)} %constant.133.cos_ref, f32[512,128]{1,0:T(8,128)} %constant.134.low_ref, f32[512,128]{1,0:T(8,128)} %constant.135.high_ref, ...), custom_call_target="tpu_custom_call" | custom-call | tf_op jit(solution)/shard_map/attention/pallas_call | solution.py:444
  243.6 16.4 %attention_grads.1 = (bf16[512,1024]{1,0:T(8,128)(2,1)}, bf16[512,1024]{1,0:T(8,128)(2,1)}, bf16[512,1024]{1,0:T(8,128)(2,1)}, bf16[512,1024]{1,0:T(8,128)(2,1)}) custom-call(bf16[2048,2048]{1,0:T(8,128)(2,1)} %join.2.hidden_ref, bf16[2048,2048]{1,0:T(8,128)(2,1)} %join.3.cotan_ref, bf16[2048,768]{1,0:T(8,128)(2,1)} %get-tuple-element.286.d_proj_ref.first_ref, ...), custom_call_target="tpu_custom_call" | custom-call | tf_op jit(solution)/shard_map/attention_grads/pallas_call | solution.py:488
  262.1 32.3 %fc1_pass.1 = (bf16[2048,1024]{1,0:T(8,128)(2,1)}, f32[2048,1024]{1,0:T(8,128)}, bf16[512,1024]{1,0:T(8,128)(2,1)}, bf16[512,1024]{1,0:T(8,128)(2,1)}, bf16[512,...) custom-call(bf16[2048,2048]{1,0:T(8,128)(2,1)} %join.2.hidden_ref, bf16[2048,2048]{1,0:T(8,128)(2,1)} %join.3.cotan_ref, ...), custom_call_target="tpu_custom_call" | custom-call | tf_op jit(solution)/shard_map/fc1_pass/pallas_call | solution.py:519
  296.4 10.7 %collective-permute-done.35.refs_3_.refs_7_ = bf16[512,1024]{1,0:T(8,128)(2,1)S(1)} collective-permute-done((bf16[512,1024]{1,0:T(8,128)(2,1)S(1)}, bf16[512,1024]{1,0:T(8,128)(2,1)S(1)}, u32[]{:S(2)}, u32[]{:S(2)}) %collective-permute-start.35) | collective-permute-done | bytes 1048608 | tf_op jit(solution)/shard_map/ppermute | solution.py:34
  309.4 28.1 %fc2_pass.1 = (bf16[2048,1024]{1,0:T(8,128)(2,1)}, bf16[512,1024]{1,0:T(8,128)(2,1)}, bf16[512,1024]{1,0:T(8,128)(2,1)}, bf16[512,1024]{1,0:T(8,128)(2,1)}, bf16[512,1024]{1,0:T(8,128)(2,1)}) custom-call(bf16[2048,2048]{1,0:T(8,128)(2,1)} %join.2.hidden_ref, bf16[2048,2048]{1,0:T(8,128)(2,1)} %join.3.cotan_ref, f32[2048,1024]{1,0:T(8,128)} %get-tuple-element.289.slope_ref, ...), custom_call_target="tpu_custom_call" | custom-call | tf_op jit(solution)/shard_map/fc2_pass/pallas_call | solution.py:553
  337.5 26.8 %back_product.2 = (bf16[1024,2048]{1,0:T(8,128)(2,1)}, bf16[1024,2048]{1,0:T(8,128)(2,1)}) custom-call(s32[17]{0:T(128)} %stack.130.table_ref, bf16[2048,768]{1,0:T(8,128)(2,1)} %get-tuple-element.286.d_proj_ref.first_ref, bf16[2048,1024]{1,0:T(8,128)(2,1)} %get-tuple-element.290.second_ref, bf16[512,1024]{1,0:T(8,128)(2,1)} %copy-done.1, ...), custom_call_target="tpu_custom_call" | custom-call | tf_op jit(solution)/shard_map/back_product/pallas_call | solution.py:600
  381.7 10.0 %collective-permute-done.40 = bf16[512,1024]{1,0:T(8,128)(2,1)S(1)} collective-permute-done((bf16[512,1024]{1,0:T(8,128)(2,1)S(1)}, bf16[512,1024]{1,0:T(8,128)(2,1)S(1)}, u32[]{:S(2)}, u32[]{:S(2)}) %collective-permute-start.40) | collective-permute-done | bytes 1048608 | tf_op jit(solution)/shard_map/ppermute | solution.py:34
  391.6 22.2 %back_product.3 = (bf16[1024,2048]{1,0:T(8,128)(2,1)}, bf16[1024,2048]{1,0:T(8,128)(2,1)}) custom-call(s32[17]{0:T(128)} %stack.130.table_ref, bf16[2048,256]{1,0:T(8,128)(2,1)} %get-tuple-element.312.context_ref.first_ref, bf16[2048,1024]{1,0:T(8,128)(2,1)} %get-tuple-element.313.second_ref, bf16[512,1024]{1,0:T(8,128)(2,1)} %copy-done.1, ...), custom_call_target="tpu_custom_call" | custom-call | tf_op jit(solution)/shard_map/back_product/pallas_call | solution.py:600
  414.3 6.3 %collective-permute-done.47 = bf16[128,1024]{1,0:T(8,128)(2,1)S(1)} collective-permute-done((bf16[128,1024]{1,0:T(8,128)(2,1)}, bf16[128,1024]{1,0:T(8,128)(2,1)S(1)}, u32[]{:S(2)}, u32[]{:S(2)}) %collective-permute-start.47) | collective-permute-done | bytes 262176 | tf_op jit(solution)/shard_map/ppermute | solution.py:38
  436.6 14.8 %collective-permute-done.55 = bf16[128,1024]{1,0:T(8,128)(2,1)} collective-permute-done((bf16[128,1024]{1,0:T(8,128)(2,1)}, bf16[128,1024]{1,0:T(8,128)(2,1)}, u32[]{:S(2)}, u32[]{:S(2)}) %collective-permute-start.55) | collective-permute-done | bytes 262176 | tf_op jit(solution)/shard_map/ppermute | solution.py:38
  462.2 7.9 %collective-permute-done.48 = bf16[512,1024]{1,0:T(8,128)(2,1)S(1)} collective-permute-done((bf16[512,1024]{1,0:T(8,128)(2,1)S(1)}, bf16[512,1024]{1,0:T(8,128)(2,1)S(1)}, u32[]{:S(2)}, u32[]{:S(2)}) %collective-permute-start.48) | collective-permute-done | bytes 1048608 | tf_op jit(solution)/shard_map/ppermute | solution.py:43
  470.2 22.3 %collective-permute-done.51 = bf16[256,2048]{1,0:T(8,128)(2,1)S(1)} collective-permute-done((bf16[256,2048]{1,0:T(8,128)(2,1)S(1)}, bf16[256,2048]{1,0:T(8,128)(2,1)S(1)}, u32[]{:S(2)}, u32[]{:S(2)}) %collective-permute-start.51) | collective-permute-done | bytes 1048608 | tf_op jit(solution)/shard_map/ppermute | solution.py:34
  515.3 10.0 %collective-permute-done.60 = f32[2,2048]{1,0:T(2,128)S(1)} collective-permute-done((f32[2,2048]{1,0:T(2,128)S(1)}, f32[2,2048]{1,0:T(2,128)S(1)}, u32[]{:S(2)}, u32[]{:S(2)}) %collective-permute-start.60) | collective-permute-done | bytes 16416 | tf_op jit(solution)/shard_map/ppermute | solution.py:34
  530.9 7.0 %add_multiply_fusion = (f32[128,4096]{1,0:T(8,128)}, f32[128,4096]{1,0:T(8,128)}, f32[128,4096]{1,0:T(8,128)}, f32[128,4096]{1,0:T(8,128)}) fusion(bf16[128,4096]{1,0:T(8,128)(2,1)} %param.28, f32[128,4096]{1,0:T(8,128)} %param.40, f32[128,4096]{1,0:T(8,128)} %param.41, bf16[128,4096]{1,0:T(8,128)(2,1)} %constant_dynamic-update-slice_fusion), kind=kLoop, calls=%fused_computation.20 | loop fusion | flops 8388608 | bytes 14680064 | tf_op jit(solution)/shard_map/mul | solution.py:637
  (316 shorter events, 172.0 us)
Async XLA Ops:
  4.5 43.1 %collective-permute-start.3 = (bf16[256,2048]{1,0:T(8,128)(2,1)}, bf16[256,2048]{1,0:T(8,128)(2,1)S(1)}, u32[]{:S(2)}, u32[]{:S(2)}) collective-permute-start(bf16[256,2048]{1,0:T(8,128)(2,1)} %refs_0_), channel_id=1, source_target_pairs={{0,1},{1,0},{2,3},{3,2},{4,5},{5,4},{6,7},{7,6},{8,9},{9,8},{10,11... | collective-permute-start | bytes 3145736 | tf_op jit(solution)/shard_map/ppermute | solution.py:34
  6.0 41.7 %collective-permute-start.4 = (bf16[256,2048]{1,0:T(8,128)(2,1)}, bf16[256,2048]{1,0:T(8,128)(2,1)S(1)}, u32[]{:S(2)}, u32[]{:S(2)}) collective-permute-start(bf16[256,2048]{1,0:T(8,128)(2,1)} %refs_0_), channel_id=1, source_target_pairs={{0,8},{8,0},{1,9},{9,1},{2,10},{10,2},{3,11},{11,3},{4,12},{12,4},... | collective-permute-start | bytes 3145736 | tf_op jit(solution)/shard_map/ppermute | solution.py:34
  6.4 41.2 %collective-permute-start.5 = (bf16[256,2048]{1,0:T(8,128)(2,1)}, bf16[256,2048]{1,0:T(8,128)(2,1)}, u32[]{:S(2)}, u32[]{:S(2)}) collective-permute-start(bf16[256,2048]{1,0:T(8,128)(2,1)} %refs_0_), channel_id=1, source_target_pairs={{0,2},{2,0},{1,3},{3,1},{4,6},{6,4},{5,7},{7,5},{8,10},{10,8},{9,1... | collective-permute-start | bytes 3145736 | tf_op jit(solution)/shard_map/ppermute | solution.py:34
  6.4 42.2 %collective-permute-start.6 = (bf16[256,2048]{1,0:T(8,128)(2,1)}, bf16[256,2048]{1,0:T(8,128)(2,1)}, u32[]{:S(2)}, u32[]{:S(2)}) collective-permute-start(bf16[256,2048]{1,0:T(8,128)(2,1)} %refs_0_.1), channel_id=1, source_target_pairs={{0,2},{2,0},{1,3},{3,1},{4,6},{6,4},{5,7},{7,5},{8,10},{10,8},{9,1... | collective-permute-start | bytes 3145736 | tf_op jit(solution)/shard_map/ppermute | solution.py:34
  49.0 48.7 %collective-permute-start.11 = (bf16[512,1024]{1,0:T(8,128)(2,1)S(1)}, bf16[512,1024]{1,0:T(8,128)(2,1)S(1)}, u32[]{:S(2)}, u32[]{:S(2)}) collective-permute-start(bf16[512,1024]{1,0:T(8,128)(2,1)S(1)} %pad_maximum_fusion.refs_0_), channel_id=1, source_target_pairs={{0,16},{16,0},{1,17},{17,1},{2,18},{18,2},{3,19},{19,3},{4,20},{20... | collective-permute-start | bytes 3145736 | tf_op jit(solution)/shard_map/ppermute | solution.py:43
  50.7 46.9 %collective-permute-start.12 = (bf16[512,1024]{1,0:T(8,128)(2,1)S(1)}, bf16[512,1024]{1,0:T(8,128)(2,1)S(1)}, u32[]{:S(2)}, u32[]{:S(2)}) collective-permute-start(bf16[512,1024]{1,0:T(8,128)(2,1)S(1)} %pad_maximum_fusion.refs_0_), channel_id=1, source_target_pairs={{0,4},{4,0},{1,5},{5,1},{2,6},{6,2},{3,7},{7,3},{8,12},{12,8},{9,1... | collective-permute-start | bytes 3145736 | tf_op jit(solution)/shard_map/ppermute | solution.py:34
  52.3 45.9 %collective-permute-start.16 = (bf16[256,2048]{1,0:T(8,128)(2,1)}, bf16[256,2048]{1,0:T(8,128)(2,1)}, u32[]{:S(2)}, u32[]{:S(2)}) collective-permute-start(bf16[256,2048]{1,0:T(8,128)(2,1)} %copy-done.22), channel_id=1, source_target_pairs={{0,1},{1,0},{2,3},{3,2},{4,5},{5,4},{6,7},{7,6},{8,9},{9,8},{10,11... | collective-permute-start | bytes 3145736 | tf_op jit(solution)/shard_map/ppermute | solution.py:34
  120.2 48.5 %collective-permute-start.22 = (bf16[512,1024]{1,0:T(8,128)(2,1)S(1)}, bf16[512,1024]{1,0:T(8,128)(2,1)S(1)}, u32[]{:S(2)}, u32[]{:S(2)}) collective-permute-start(bf16[512,1024]{1,0:T(8,128)(2,1)S(1)} %pad_maximum_fusion.1.refs_0_.refs_4_), channel_id=1, source_target_pairs={{0,16},{16,0},{1,17},{17,1},{2,18},{18,2},{3,19},{19,3},{4,20},{20... | collective-permute-start | bytes 3145736 | tf_op jit(solution)/shard_map/ppermute | solution.py:43
  120.9 47.8 %collective-permute-start.28 = (bf16[256,2048]{1,0:T(8,128)(2,1)}, bf16[256,2048]{1,0:T(8,128)(2,1)}, u32[]{:S(2)}, u32[]{:S(2)}) collective-permute-start(bf16[256,2048]{1,0:T(8,128)(2,1)} %collective-permute-done.18.refs_2_), channel_id=1, source_target_pairs={{0,1},{1,0},{2,3},{3,2},{4,5},{5,4},{6,7},{7,6},{8,9},{9,8},{10,11... | collective-permute-start | bytes 3145736 | tf_op jit(solution)/shard_map/ppermute | solution.py:34
  154.8 41.2 %collective-permute-start.30 = (bf16[256,2048]{1,0:T(8,128)(2,1)}, bf16[256,2048]{1,0:T(8,128)(2,1)}, u32[]{:S(2)}, u32[]{:S(2)}) collective-permute-start(bf16[256,2048]{1,0:T(8,128)(2,1)} %collective-permute-done.18.refs_2_), channel_id=1, source_target_pairs={{0,2},{2,0},{1,3},{3,1},{4,6},{6,4},{5,7},{7,5},{8,10},{10,8},{9,1... | collective-permute-start | bytes 3145736 | tf_op jit(solution)/shard_map/ppermute | solution.py:34
  154.8 41.2 %collective-permute-start.24 = (bf16[512,1024]{1,0:T(8,128)(2,1)S(1)}, bf16[512,1024]{1,0:T(8,128)(2,1)}, u32[]{:S(2)}, u32[]{:S(2)}) collective-permute-start(bf16[512,1024]{1,0:T(8,128)(2,1)S(1)} %collective-permute-done.11.refs_1_), channel_id=1, source_target_pairs={{0,4},{4,0},{1,5},{5,1},{2,6},{6,2},{3,7},{7,3},{8,12},{12,8},{9,1... | collective-permute-start | bytes 3145736 | tf_op jit(solution)/shard_map/ppermute | solution.py:34
  196.0 64.0 %collective-permute-start.32 = (bf16[512,1024]{1,0:T(8,128)(2,1)S(1)}, bf16[512,1024]{1,0:T(8,128)(2,1)S(1)}, u32[]{:S(2)}, u32[]{:S(2)}) collective-permute-start(bf16[512,1024]{1,0:T(8,128)(2,1)S(1)} %collective-permute-done.22.refs_1_.refs_5_), channel_id=1, source_target_pairs={{0,4},{4,0},{1,5},{5,1},{2,6},{6,2},{3,7},{7,3},{8,12},{12,8},{9,1... | collective-permute-start | bytes 3145736 | tf_op jit(solution)/shard_map/ppermute | solution.py:34
  197.6 62.4 %collective-permute-start.33 = (bf16[512,1024]{1,0:T(8,128)(2,1)S(1)}, bf16[512,1024]{1,0:T(8,128)(2,1)S(1)}, u32[]{:S(2)}, u32[]{:S(2)}) collective-permute-start(bf16[512,1024]{1,0:T(8,128)(2,1)S(1)} %pad_maximum_fusion.2.refs_0_.refs_4_), channel_id=1, source_target_pairs={{0,16},{16,0},{1,17},{17,1},{2,18},{18,2},{3,19},{19,3},{4,20},{20... | collective-permute-start | bytes 3145736 | tf_op jit(solution)/shard_map/ppermute | solution.py:43
  202.0 58.0 %collective-permute-start.34 = (bf16[512,1024]{1,0:T(8,128)(2,1)S(1)}, bf16[512,1024]{1,0:T(8,128)(2,1)S(1)}, u32[]{:S(2)}, u32[]{:S(2)}) collective-permute-start(bf16[512,1024]{1,0:T(8,128)(2,1)S(1)} %pad_maximum_fusion.2.refs_0_.refs_4_), channel_id=1, source_target_pairs={{0,4},{4,0},{1,5},{5,1},{2,6},{6,2},{3,7},{7,3},{8,12},{12,8},{9,1... | collective-permute-start | bytes 3145736 | tf_op jit(solution)/shard_map/ppermute | solution.py:34
  261.7 45.4 %collective-permute-start.35 = (bf16[512,1024]{1,0:T(8,128)(2,1)S(1)}, bf16[512,1024]{1,0:T(8,128)(2,1)S(1)}, u32[]{:S(2)}, u32[]{:S(2)}) collective-permute-start(bf16[512,1024]{1,0:T(8,128)(2,1)S(1)} %collective-permute-done.33.refs_1_.refs_5_), channel_id=1, source_target_pairs={{0,4},{4,0},{1,5},{5,1},{2,6},{6,2},{3,7},{7,3},{8,12},{12,8},{9,1... | collective-permute-start | bytes 3145736 | tf_op jit(solution)/shard_map/ppermute | solution.py:34
  307.1 57.2 %collective-permute-start.39 = (bf16[512,1024]{1,0:T(8,128)(2,1)}, bf16[512,1024]{1,0:T(8,128)(2,1)S(1)}, u32[]{:S(2)}, u32[]{:S(2)}) collective-permute-start(bf16[512,1024]{1,0:T(8,128)(2,1)} %get-tuple-element.283), channel_id=1, source_target_pairs={{0,4},{4,0},{1,5},{5,1},{2,6},{6,2},{3,7},{7,3},{8,12},{12,8},{9,1... | collective-permute-start | bytes 3145736 | tf_op jit(solution)/shard_map/ppermute | solution.py:34
  308.7 56.1 %collective-permute-start.37 = (bf16[512,1024]{1,0:T(8,128)(2,1)S(1)}, bf16[512,1024]{1,0:T(8,128)(2,1)}, u32[]{:S(2)}, u32[]{:S(2)}) collective-permute-start(bf16[512,1024]{1,0:T(8,128)(2,1)S(1)} %add.496), channel_id=1, source_target_pairs={{0,16},{16,0},{1,17},{17,1},{2,18},{18,2},{3,19},{19,3},{4,20},{20... | collective-permute-start | bytes 3145736 | tf_op jit(solution)/shard_map/ppermute | solution.py:43
  308.9 55.9 %collective-permute-start.38 = (bf16[512,1024]{1,0:T(8,128)(2,1)}, bf16[512,1024]{1,0:T(8,128)(2,1)}, u32[]{:S(2)}, u32[]{:S(2)}) collective-permute-start(bf16[512,1024]{1,0:T(8,128)(2,1)} %get-tuple-element.281), channel_id=1, source_target_pairs={{0,4},{4,0},{1,5},{5,1},{2,6},{6,2},{3,7},{7,3},{8,12},{12,8},{9,1... | collective-permute-start | bytes 3145736 | tf_op jit(solution)/shard_map/ppermute | solution.py:34
  367.1 53.5 %collective-permute-start.41 = (bf16[512,1024]{1,0:T(8,128)(2,1)S(1)}, bf16[512,1024]{1,0:T(8,128)(2,1)}, u32[]{:S(2)}, u32[]{:S(2)}) collective-permute-start(bf16[512,1024]{1,0:T(8,128)(2,1)S(1)} %add.497), channel_id=1, source_target_pairs={{0,16},{16,0},{1,17},{17,1},{2,18},{18,2},{3,19},{19,3},{4,20},{20... | collective-permute-start | bytes 3145736 | tf_op jit(solution)/shard_map/ppermute | solution.py:43
  369.7 51.5 %collective-permute-start.42 = (bf16[512,1024]{1,0:T(8,128)(2,1)}, bf16[512,1024]{1,0:T(8,128)(2,1)}, u32[]{:S(2)}, u32[]{:S(2)}) collective-permute-start(bf16[512,1024]{1,0:T(8,128)(2,1)} %get-tuple-element.309), channel_id=1, source_target_pairs={{0,4},{4,0},{1,5},{5,1},{2,6},{6,2},{3,7},{7,3},{8,12},{12,8},{9,1... | collective-permute-start | bytes 3145736 | tf_op jit(solution)/shard_map/ppermute | solution.py:34
  375.3 46.0 %collective-permute-start.44 = (bf16[256,2048]{1,0:T(8,128)(2,1)}, bf16[256,2048]{1,0:T(8,128)(2,1)}, u32[]{:S(2)}, u32[]{:S(2)}) collective-permute-start(bf16[256,2048]{1,0:T(8,128)(2,1)} %dynamic-slice_add_fusion.3), channel_id=1, source_target_pairs={{0,1},{1,0},{2,3},{3,2},{4,5},{5,4},{6,7},{7,6},{8,9},{9,8},{10,11... | collective-permute-start | bytes 3145736 | tf_op jit(solution)/shard_map/ppermute | solution.py:34
  422.1 48.1 %collective-permute-start.48 = (bf16[512,1024]{1,0:T(8,128)(2,1)S(1)}, bf16[512,1024]{1,0:T(8,128)(2,1)S(1)}, u32[]{:S(2)}, u32[]{:S(2)}) collective-permute-start(bf16[512,1024]{1,0:T(8,128)(2,1)S(1)} %add.498), channel_id=1, source_target_pairs={{0,16},{16,0},{1,17},{17,1},{2,18},{18,2},{3,19},{19,3},{4,20},{20... | collective-permute-start | bytes 3145736 | tf_op jit(solution)/shard_map/ppermute | solution.py:43
  499.5 56.7 %collective-permute-start.58 = (bf16[256,2048]{1,0:T(8,128)(2,1)}, bf16[256,2048]{1,0:T(8,128)(2,1)}, u32[]{:S(2)}, u32[]{:S(2)}) collective-permute-start(bf16[256,2048]{1,0:T(8,128)(2,1)} %get-tuple-element.394), channel_id=1, source_target_pairs={{0,8},{8,0},{1,9},{9,1},{2,10},{10,2},{3,11},{11,3},{4,12},{12,4},... | collective-permute-start | bytes 3145736 | tf_op jit(solution)/shard_map/ppermute | solution.py:34
  499.6 56.7 %collective-permute-start.57 = (bf16[256,2048]{1,0:T(8,128)(2,1)}, bf16[256,2048]{1,0:T(8,128)(2,1)}, u32[]{:S(2)}, u32[]{:S(2)}) collective-permute-start(bf16[256,2048]{1,0:T(8,128)(2,1)} %get-tuple-element.393), channel_id=1, source_target_pairs={{0,1},{1,0},{2,3},{3,2},{4,5},{5,4},{6,7},{7,6},{8,9},{9,8},{10,11... | collective-permute-start | bytes 3145736 | tf_op jit(solution)/shard_map/ppermute | solution.py:34
  (106 other events, 2059.3 us)

commit v3 on v2

--- a/solution.py
+++ b/solution.py
@@ -74,10 +74,13 @@
     return jnp.concatenate([qkv[0], qkv[1], qkv[2], column_block(out_weight, j)], axis=1)
 
 
-def spread(piece_of):
+def cut(piece_of):
     r = inner_index()
-    pieces = [swap_inner(piece_of(r ^ flip), flip) for flip in range(1, 4)]
-    return jnp.concatenate([piece_of(r), *pieces])
+    return [piece_of(r ^ flip) for flip in range(4)]
+
+
+def exchange(pieces):
+    return [pieces[0]] + [swap_inner(piece, flip) for flip, piece in enumerate(pieces[1:], 1)]
 
 
 def collect(total):
@@ -185,30 +188,28 @@
     return out
 
 
-def flips_outer(value):
-    n = lax.axis_size("h")
-    bit = 1
-    while bit < n:
-        value = value + lax.ppermute(value, "h", [(i, i ^ bit) for i in range(n)])
-        bit *= 2
-    return value
-
-
-def gather_vectors(pair):
-    count = 8 * lax.axis_size("h")
-    out = jnp.zeros((2, count * pair.shape[1]), pair.dtype)
-    out = lax.dynamic_update_slice(out, pair, (0, dp_index() * pair.shape[1]))
-    for axis in "wyc":
-        out = out + swap(out, axis)
-    return flips_outer(out)
-
-
-def sum_vectors(pair):
-    for axis in "ctyw":
-        pair = pair + swap(pair, axis)
-    pair = flips_outer(pair)
-    width = pair.shape[1] // (8 * lax.axis_size("h"))
-    return lax.dynamic_slice(pair, (0, dp_index() * width), (2, width))
+def shifted(value):
+    n = 2 * lax.axis_size("h")
+    return [
+        lax.ppermute(value, ("h", "w"), [(i, (i + k) % n) for i in range(n)]) for k in range(1, n)
+    ]
+
+
+def place_vectors(pair):
+    out = jnp.zeros((2, 8 * lax.axis_size("h") * pair.shape[1]), pair.dtype)
+    return lax.dynamic_update_slice(out, pair, (0, dp_index() * pair.shape[1]))
+
+
+def relative(vectors, table):
+    rows, features = vectors.shape
+    blocks = table.shape[0] - 1
+    parts = jnp.take(vectors.reshape(rows, blocks, features // blocks), table[1:], axis=1)
+    return parts.reshape(rows, features)
+
+
+def own_part(sums):
+    width = sums.shape[1] // (8 * lax.axis_size("h"))
+    return lax.dynamic_slice(sums, (0, dp_index() * width), (2, width))
 
 
 def lane_tables(length):
@@ -350,68 +351,6 @@
             copy.wait()
 
 
-def join_step(table_ref, *refs, norm, permute):
-    pieces, (gain_ref, bias_ref, out_ref, buffer, sems) = refs[:8], refs[8:]
-    step = pl.program_id(0)
-    features = out_ref.shape[1]
-    blocks = table_ref.shape[0] - 1 if permute else 1
-    size = features // blocks
-
-    def copy(i, slot):
-        return pltpu.make_async_copy(pieces[i], buffer.at[slot], sems.at[slot])
-
-    for i in range(8):
-        pl.when(step == max(i - 1, 0))(lambda i=i: copy(i, i % 2).start())
-    slot = lax.rem(step, 2)
-    copy(0, slot).wait()
-    chunk = min(128, out_ref.shape[0])
-
-    def emit(i, carry):
-        at = pl.ds(pl.multiple_of(i * chunk, chunk), chunk)
-        if norm:
-            rows = buffer[slot, at, :].astype(F32)
-            mean = jnp.mean(rows, axis=1, keepdims=True)
-            centred = rows - mean
-            inv_std = lax.rsqrt(jnp.mean(centred * centred, axis=1, keepdims=True) + EPS_NORM)
-        for j in range(blocks):
-            lanes = pl.ds(pl.multiple_of(table_ref[1 + j] * size, size), size) if permute else slice(None)
-            value = buffer[slot, at, lanes]
-            if norm:
-                normed = (value.astype(F32) - mean) * inv_std
-                value = (normed * gain_ref[:, lanes] + bias_ref[:, lanes]).astype(BF16)
-            out_ref[at, j * size : (j + 1) * size] = value
-        return carry
-
-    lax.fori_loop(0, out_ref.shape[0] // chunk, emit, 0)
-
-
-def join(table, pieces, gain, bias, norm):
-    block, features = pieces[0].shape
-    blocks = table.shape[0] - 1
-    permute = features // blocks % 128 == 0
-    vector = pl.BlockSpec((1, features), lambda s, h: (0, 0))
-    out = pl.pallas_call(
-        functools.partial(join_step, norm=norm, permute=permute),
-        grid_spec=pltpu.PrefetchScalarGridSpec(
-            num_scalar_prefetch=1,
-            grid=(8,),
-            in_specs=[ANYWHERE] * 8 + [vector, vector],
-            out_specs=pl.BlockSpec((block, features), lambda s, h: (s - s % 2 + (s + h[0]) % 2, 0)),
-            scratch_shapes=[
-                pltpu.VMEM((2, block, features), BF16),
-                pltpu.SemaphoreType.DMA((2,)),
-            ],
-        ),
-        out_shape=jax.ShapeDtypeStruct((8 * block, features), BF16),
-        compiler_params=PARAMS,
-        name="join",
-    )(table, *pieces, gain, bias)
-    if not permute:
-        cut = out.reshape(8 * block, blocks, features // blocks)
-        out = jnp.take(cut, table[1:], axis=1).reshape(8 * block, features)
-    return out
-
-
 def add_and_flush(total_ref, part_refs, addends):
     step = pl.program_id(0)
 
@@ -429,38 +368,104 @@
             part_ref[...] = total_ref[i * rows : (i + 1) * rows, :].astype(BF16)
 
 
-def attention_step(hidden_ref, cotan_ref, cos_ref, low_ref, high_ref, *refs):
-    pieces, (context_ref, d_proj_ref, cols_ref, proj_ref, grad_ref, sems) = refs[:-6], refs[-6:]
+def attention_step(table_ref, gain_ref, bias_ref, cos_ref, low_ref, high_ref, *refs, permute):
+    x_pieces, g_pieces, pieces, refs = refs[:8], refs[8:16], refs[16:-12], refs[-12:]
+    context_ref, d_proj_ref, hidden_ref, cotan_ref, cols_ref, proj_ref, grad_ref = refs[:7]
+    x_buffer, g_buffer, x_sems, g_sems, sems = refs[7:]
+    step = pl.program_id(0)
+    length, features = hidden_ref.shape
+    half = length // 2
+    blocks = table_ref.shape[0] - 1 if permute else 1
+    size = features // blocks
+
+    def start(sequence):
+        slot = sequence % 2
+        for i in range(2):
+            side = table_ref[0] if i == 0 else 1 - table_ref[0]
+            rows = pl.ds(pl.multiple_of(side * half, half), half)
+
+            def block(j, carry, i=i, rows=rows):
+                entry = table_ref[1 + j] if permute else 0
+                of = pl.ds(pl.multiple_of(entry * size, size), size)
+                to = pl.ds(pl.multiple_of(j * size, size), size)
+                for sources, buffer, buffer_sems in (
+                    (x_pieces, x_buffer, x_sems),
+                    (g_pieces, g_buffer, g_sems),
+                ):
+                    pltpu.make_async_copy(
+                        sources[2 * sequence + i].at[:, of],
+                        buffer.at[slot, rows, to],
+                        buffer_sems.at[slot],
+                    ).start()
+                return carry
+
+            lax.fori_loop(0, blocks, block, 0)
+
+    pl.when(step == 0)(lambda: start(0))
+    for sequence in range(1, 4):
+        pl.when(step == sequence - 1)(lambda sequence=sequence: start(sequence))
     fetch(pieces, cols_ref, sems)
+    slot = lax.rem(step, 2)
+    for buffer, buffer_sems in ((x_buffer, x_sems), (g_buffer, g_sems)):
+        pltpu.make_async_copy(buffer.at[slot], buffer.at[slot], buffer_sems.at[slot]).wait()
+    chunk = min(128, length)
+
+    def normalize(i, carry):
+        at = pl.ds(pl.multiple_of(i * chunk, chunk), chunk)
+        rows = x_buffer[slot, at, :].astype(F32)
+        centred = rows - jnp.mean(rows, axis=1, keepdims=True)
+        inv_std = lax.rsqrt(jnp.mean(centred * centred, axis=1, keepdims=True) + EPS_NORM)
+        hidden_ref[at, :] = (centred * inv_std * gain_ref[...] + bias_ref[...]).astype(BF16)
+        return carry
+
+    lax.fori_loop(0, length // chunk, normalize, 0)
+    cotan_ref[...] = g_buffer[slot]
     width = grad_ref.shape[1]
     proj_ref[...] = dot_nn(hidden_ref[...], cols_ref[:, : 3 * width])
     grad_ref[...] = dot_nn(cotan_ref[...], cols_ref[:, 3 * width :]).astype(BF16)
     attention_body(proj_ref, grad_ref, cos_ref, low_ref, high_ref, context_ref, d_proj_ref)
 
 
-def attention(hidden, cotan, pieces, length):
-    tokens, features = hidden.shape
+def attention(table, x_pieces, g_pieces, gain, bias, pieces):
+    half, features = x_pieces[0].shape
+    length, tokens = 2 * half, 8 * half
     width = pieces[0].shape[1] // 4
+    permute = features // (table.shape[0] - 1) % 128 == 0
+    if not permute:
+        x_pieces = [relative(piece, table) for piece in x_pieces]
+        g_pieces = [relative(piece, table) for piece in g_pieces]
+
+    def rows(columns):
+        return pl.BlockSpec((length, columns), lambda s, h: (s, 0))
+
+    def fixed(shape):
+        return pl.BlockSpec(shape, lambda s, h: (0, 0), pipeline_mode=pl.Buffered(1))
+
+    widths = (width, 3 * width, features, features)
     return pl.pallas_call(
-        attention_step,
-        grid=(tokens // length,),
-        in_specs=[rows_of(length, features)] * 2
-        + [whole((length, PAIR))] * 3
-        + [ANYWHERE] * len(pieces),
-        out_specs=(rows_of(length, width), rows_of(length, 3 * width)),
-        out_shape=(
-            jax.ShapeDtypeStruct((tokens, width), BF16),
-            jax.ShapeDtypeStruct((tokens, 3 * width), BF16),
+        functools.partial(attention_step, permute=permute),
+        grid_spec=pltpu.PrefetchScalarGridSpec(
+            num_scalar_prefetch=1,
+            grid=(4,),
+            in_specs=[fixed((1, features))] * 2
+            + [fixed((length, PAIR))] * 3
+            + [ANYWHERE] * (16 + len(pieces)),
+            out_specs=[rows(columns) for columns in widths],
+            scratch_shapes=[
+                pltpu.VMEM((features, 4 * width), BF16),
+                pltpu.VMEM((length, 3 * width), F32),
+                pltpu.VMEM((length, width), BF16),
+                pltpu.VMEM((2, length, features), BF16),
+                pltpu.VMEM((2, length, features), BF16),
+                pltpu.SemaphoreType.DMA((2,)),
+                pltpu.SemaphoreType.DMA((2,)),
+                pltpu.SemaphoreType.DMA((len(pieces),)),
+            ],
         ),
-        scratch_shapes=[
-            pltpu.VMEM((features, 4 * width), BF16),
-            pltpu.VMEM((length, 3 * width), F32),
-            pltpu.VMEM((length, width), BF16),
-            pltpu.SemaphoreType.DMA((len(pieces),)),
-        ],
+        out_shape=[jax.ShapeDtypeStruct((tokens, columns), BF16) for columns in widths],
         compiler_params=PARAMS,
         name="attention",
-    )(hidden, cotan, *lane_tables(length), *pieces)
+    )(table, gain, bias, *lane_tables(length), *x_pieces, *g_pieces, *pieces)
 
 
 def parts_of(count, features, width):
@@ -665,34 +670,54 @@
     count = 2 * lax.axis_size("h")
     table = feature_table()
 
-    attn = Gather(spread(functools.partial(attention_block, qkv_weight, out_weight)))
+    first = exchange(
+        cut(
+            lambda j: jnp.concatenate(
+                [attention_block(qkv_weight, out_weight, j), column_block(fc1_weight, j)], axis=1
+            )
+        )
+    )
+    fc2_cut = cut(functools.partial(column_block, fc2_weight))
     x, g = [inputs, swap(inputs, "t"), swap(inputs, "w")], [cotangent]
-    x_other, g_other = [swap(inputs, "c")], [swap(cotangent, "c")]
-    vectors = gather_vectors(jnp.stack([ln_gain, ln_bias]))
-    x, g, x_other, g_other, vectors, fc1_late, fc2_late = close(attn, x, g, x_other, g_other, vectors, fc1_weight, fc2_weight)
+    vectors = place_vectors(jnp.stack([ln_gain, ln_bias]))
+    vectors = vectors + swap(vectors, "y")
+    vectors = vectors + swap(vectors, "c")
+    first, x, g, fc2_cut, vectors = close(first, x, g, fc2_cut, vectors)
+    split = 4 * (qkv_weight.shape[2] // 4)
+    attn = Gather(jnp.concatenate([piece[:, :split] for piece in first]))
     attn.over_h()
     attn.over_y_first()
+    others = shifted(vectors)
+    x_other = [swap(piece, "c") for piece in x]
+    x.append(swap(x[2], "t"))
     g += [swap(g[0], "t"), swap(g[0], "w")]
-    x.append(swap(x[2], "t"))
-    x_other += [swap(x[1], "c"), swap(x[2], "c"), swap(x[3], "c")]
-    fc1 = Gather(spread(functools.partial(column_block, fc1_late)))
-    x, g, x_other, g_other, vectors, fc2_late = close(attn, fc1, x, g, x_other, g_other, vectors, fc2_late)
+    fc1 = Gather(jnp.concatenate([piece[:, split:] for piece in first]))
+    others, x_other, x, g, fc2_cut, vectors = close(
+        others, x_other, attn, x, g, fc2_cut, fc1, vectors
+    )
+    vectors = sum(others, vectors)
+    fc2 = Gather(jnp.concatenate(exchange(fc2_cut)))
     fc1.over_h()
+    attn.over_y_rest()
     fc1.over_y_first()
-    attn.over_y_rest()
     g.append(swap(g[2], "t"))
-    g_other += [swap(g[1], "c"), swap(g[2], "c"), swap(g[3], "c")]
-    gain_wide, bias_wide = vectors[:1].astype(F32), vectors[1:].astype(F32)
-    fc2 = Gather(spread(functools.partial(column_block, fc2_late)))
-    hidden = join(table, x + x_other, gain_wide, bias_wide, True)
-    g, g_other, hidden = close(fc1, attn, fc2, g, g_other, hidden)
+    x_late = swap(x[3], "c")
+    g_other = [swap(piece, "c") for piece in g]
+    g, x, x_other, x_late, g_other, vectors = close(
+        fc1, attn, g, fc2, x, x_other, x_late, g_other, vectors
+    )
+    x_other.append(x_late)
     fc2.over_h()
     fc2.over_y_first()
     fc1.over_y_rest()
-    cotan = join(table, g + g_other, gain_wide, bias_wide, False)
-    context, d_proj = attention(hidden, cotan, attn.pieces(), length)
+    affine = relative(vectors, table).astype(F32)
+    context, d_proj, hidden, cotan = attention(
+        table, x + x_other, g + g_other, affine[:1], affine[1:], attn.pieces()
+    )
     attn_parts = attention_grads(hidden, cotan, d_proj, context, block, count)
-    hidden, cotan, context, d_proj, attn_parts = close(attn, fc1, fc2, hidden, cotan, context, d_proj, attn_parts)
+    hidden, cotan, context, d_proj, attn_parts = close(
+        attn, fc1, fc2, hidden, cotan, context, d_proj, attn_parts
+    )
     fc2.over_y_rest()
     attn_sum = Reduce(attn_parts)
     attn_sum.over_y_rest()
@@ -723,28 +748,33 @@
     qkv_grad, out_grad = join_attention(attn_pieces)
     qkv_res = adamw(qkv_weight, qkv_grad, m_qkv, v_qkv)
     out_res = adamw(out_weight, out_grad, m_out, v_out)
-    fc2_pieces = collect(fc2_sum.total())
-    (fc2_pieces,) = close(fc1_sum, d_hidden, branch, fc2_pieces)
-    branch.edges()
-    fc1_res = adamw(fc1_weight, join_columns(collect(fc1_sum.total())), m_fc1, v_fc1)
-    fc2_res = adamw(fc2_weight, join_columns(fc2_pieces), m_fc2, v_fc2)
+    fc2_total = fc2_sum.total()
+    (fc2_total,) = close(fc1_sum, d_hidden, branch, fc2_total)
+    fc1_pieces, fc2_pieces = collect(fc1_sum.total()), collect(fc2_total)
     d_hidden = d_hidden.total()
     own_rows = inputs.astype(F32)
-    output = (own_rows + branch.total()).astype(BF16)
-
     centred = own_rows - jnp.mean(own_rows, axis=1, keepdims=True)
     inv_std = lax.rsqrt(jnp.mean(centred * centred, axis=1, keepdims=True) + EPS_NORM)
     normed = centred * inv_std
-    vector_parts = jnp.stack([jnp.sum(d_hidden * normed, axis=0), jnp.sum(d_hidden, axis=0)])
-    vector_grads = sum_vectors(vector_parts)
+    sums = jnp.stack([jnp.sum(d_hidden * normed, axis=0), jnp.sum(d_hidden, axis=0)])
+    for axis in "cyt":
+        sums = sums + swap(sums, axis)
     scaled_grad = d_hidden * vectors[:1].astype(F32)
     input_grad = cotangent.astype(F32) + inv_std * (
         scaled_grad
         - jnp.mean(scaled_grad, axis=1, keepdims=True)
         - normed * jnp.mean(scaled_grad * normed, axis=1, keepdims=True)
     )
-    gain_res = adamw(ln_gain, vector_grads[0], m_gain, v_gain)
-    bias_res = adamw(ln_bias, vector_grads[1], m_bias, v_bias)
+    fc1_pieces, fc2_pieces, sums, input_grad = close(fc1_pieces, fc2_pieces, branch, sums, input_grad)
+    others = shifted(sums)
+    branch.edges()
+    fc1_res = adamw(fc1_weight, join_columns(fc1_pieces), m_fc1, v_fc1)
+    fc2_res = adamw(fc2_weight, join_columns(fc2_pieces), m_fc2, v_fc2)
+    others, fc1_res, fc2_res, sums = close(others, branch, fc1_res, fc2_res, sums)
+    output = (own_rows + branch.total()).astype(BF16)
+    sums = own_part(sum(others, sums))
+    gain_res = adamw(ln_gain, sums[0], m_gain, v_gain)
+    bias_res = adamw(ln_bias, sums[1], m_bias, v_bias)
     return (
         output,
         input_grad,

time: 566 us -> 526 us (0.929); the launches traced: 562 us -> 516 us
  waiting for transfers between devices: 237 us -> 214 us
  Pallas kernels: 181 us -> 165 us
  starting transfers between devices: 64.5 us -> 55.5 us
    ppermute x6, waiting for transfers between devices: 30.1 us -> 66.8 us  [ring(): return lax.ppermute(value, 'h', [(i, (i + 1) % n) for i in range(n)])]
    ppermute x41 -> x39, waiting for transfers between devices: 89.7 us -> 53.6 us  [swap(): return lax.ppermute(value, axis, [(0, 1), (1, 0)])]
    ppermute x2 -> x6, waiting for transfers between devices: 18 us -> 0.46 us  [shifted(): lax.ppermute(value, ('h', 'w'), [(i, (i + k) % n) for i in range(n)])]
    pallas_call x3 -> x1, Pallas kernels: 55.6 us -> 39.1 us  [attention(): pl.pallas_call(functools.partial(attention_step, permute=permute), grid_s...]
    ppermute x18 -> x15, starting transfers between devices: 16.8 us -> 5.86 us  [swap_inner(): return lax.ppermute(value, ('w', 'c'), [(i, i ^ flip) for i in range(4)])]
    ppermute x2 -> x6, starting transfers between devices: 2.73 us -> 10.4 us  [shifted(): lax.ppermute(value, ('h', 'w'), [(i, (i + k) % n) for i in range(n)])]
    convert_element_type x1 -> x4, other arithmetic: 0.62 us -> 6.83 us  [the longest x1 3.76 us: shards(): output = (own_rows + branch.total()).astype(BF16)]
    add x1 -> x2, other arithmetic: 3.55 us -> 9.47 us  [edges(): self.turning = swap(self.block(1, t) + self.moving, 'w')]
  transfers between devices with their start and end apart: 67 -> 66, of which waited for: 28 -> 28; matrix products, arithmetic and copies ran while one was open for 11% -> 14% of each run, Pallas kernels for 32% -> 32%
where the time goes in v3:
time: 526 us; the launch traced here: 516 us
  waiting for transfers between devices  214 us (41%)
  Pallas kernels  165 us (31%)
  starting transfers between devices  55.5 us (11%)
  other arithmetic  54.8 us (10%)
  local copies, waits for them, and re-layouts  24.5 us (5%)
    ppermute x15, waiting for transfers between devices, swap_inner(): return lax.ppermute(value, ('w', 'c'), [(i, i ^ flip) for i in range(4)])  93.4 us
    ppermute x6, waiting for transfers between devices, ring(): return lax.ppermute(value, 'h', [(i, (i + 1) % n) for i in range(n)])  66.8 us
    ppermute x39, waiting for transfers between devices, swap(): return lax.ppermute(value, axis, [(0, 1), (1, 0)])  53.6 us
    pallas_call x2, Pallas kernels, back_product(): pl.pallas_call(functools.partial(back_step, count=count, start=start, per...  48.9 us
    pallas_call x1, Pallas kernels, attention(): pl.pallas_call(functools.partial(attention_step, permute=permute), grid_s...  39.1 us
    ppermute x39, starting transfers between devices, swap(): return lax.ppermute(value, axis, [(0, 1), (1, 0)])  33.9 us
    pallas_call x1, Pallas kernels, fc1_pass(): pl.pallas_call(functools.partial(fc1_step, count=count), grid=(tokens //...  32.4 us
    pallas_call x1, Pallas kernels, fc2_pass(): pl.pallas_call(functools.partial(fc2_step, count=count), grid=(tokens //...  28.1 us
  transfers between devices with their start and end apart: 66, of which 28 were waited for; matrix products, arithmetic and copies ran while one was open for 14% of the time, Pallas kernels for 32%

profile of v3, /device:TPU:0, one launch (start us, length us, event | category | flops | bytes accessed | tf_op | source)
XLA Modules:
  0.0 515.8 jit_solution(10363316046176428475)
XLA Ops:
  19.0 22.3 %collective-permute-done.1 = bf16[128,2048]{1,0:T(8,128)(2,1)S(1)} collective-permute-done((bf16[128,2048]{1,0:T(8,128)(2,1)}, bf16[128,2048]{1,0:T(8,128)(2,1)S(1)}, u32[]{:S(2)}, u32[]{:S(2)}) %collective-permute-start.1) | collective-permute-done | bytes 524320 | tf_op jit(solution)/shard_map/ppermute | solution.py:38
  41.2 9.0 %collective-permute-done.2 = bf16[128,2048]{1,0:T(8,128)(2,1)S(1)} collective-permute-done((bf16[128,2048]{1,0:T(8,128)(2,1)}, bf16[128,2048]{1,0:T(8,128)(2,1)S(1)}, u32[]{:S(2)}, u32[]{:S(2)}) %collective-permute-start.2) | collective-permute-done | bytes 524320 | tf_op jit(solution)/shard_map/ppermute | solution.py:38
  64.4 41.8 %collective-permute-done.13.refs_17_.refs_1_ = bf16[512,1024]{1,0:T(8,128)(2,1)S(1)} collective-permute-done((bf16[512,1024]{1,0:T(8,128)(2,1)S(1)}, bf16[512,1024]{1,0:T(8,128)(2,1)S(1)}, u32[]{:S(2)}, u32[]{:S(2)}) %collective-permute-start.13) | collective-permute-done | bytes 1048608 | tf_op jit(solution)/shard_map/ppermute | solution.py:43
  112.4 22.5 %collective-permute-done.24 = bf16[128,1024]{1,0:T(8,128)(2,1)S(1)} collective-permute-done((bf16[128,1024]{1,0:T(8,128)(2,1)S(1)}, bf16[128,1024]{1,0:T(8,128)(2,1)S(1)}, u32[]{:S(2)}, u32[]{:S(2)}) %collective-permute-start.24) | collective-permute-done | bytes 262176 | tf_op jit(solution)/shard_map/ppermute | solution.py:38
  134.9 24.4 %collective-permute-done.23 = bf16[128,1024]{1,0:T(8,128)(2,1)S(1)} collective-permute-done((bf16[128,1024]{1,0:T(8,128)(2,1)S(1)}, bf16[128,1024]{1,0:T(8,128)(2,1)S(1)}, u32[]{:S(2)}, u32[]{:S(2)}) %collective-permute-start.23) | collective-permute-done | bytes 262176 | tf_op jit(solution)/shard_map/ppermute | solution.py:38
  174.2 39.1 %attention.1 = (bf16[2048,256]{1,0:T(8,128)(2,1)}, bf16[2048,768]{1,0:T(8,128)(2,1)}, bf16[2048,2048]{1,0:T(8,128)(2,1)}, bf16[2048,2048]{1,0:T(8,128)(2,1)}) custom-call(s32[17]{0:T(128)} %stack.166.table_ref, f32[1,2048]{1,0:T(1,128)} %get-tuple-element.542.gain_ref, f32[1,2048]{1,0:T(1,128)} %get-tuple-element.541.bias_ref, ...), custom_call_target="tpu_custom_call" | custom-call | tf_op jit(solution)/shard_map/attention/pallas_call | solution.py:445
  213.3 16.4 %attention_grads.1 = (bf16[512,1024]{1,0:T(8,128)(2,1)}, bf16[512,1024]{1,0:T(8,128)(2,1)}, bf16[512,1024]{1,0:T(8,128)(2,1)}, bf16[512,1024]{1,0:T(8,128)(2,1)}) custom-call(bf16[2048,2048]{1,0:T(8,128)(2,1)} %get-tuple-element.351.hidden_ref, bf16[2048,2048]{1,0:T(8,128)(2,1)} %get-tuple-element.352.cotan_ref, ...), custom_call_target="tpu_custom_call" | custom-call | tf_op jit(solution)/shard_map/attention_grads/pallas_call | solution.py:493
  231.8 32.4 %fc1_pass.1 = (bf16[2048,1024]{1,0:T(8,128)(2,1)}, f32[2048,1024]{1,0:T(8,128)}, bf16[512,1024]{1,0:T(8,128)(2,1)}, bf16[512,1024]{1,0:T(8,128)(2,1)}, bf16[512,...) custom-call(bf16[2048,2048]{1,0:T(8,128)(2,1)} %get-tuple-element.351.hidden_ref, ...), custom_call_target="tpu_custom_call" | custom-call | tf_op jit(solution)/shard_map/fc1_pass/pallas_call | solution.py:524
  264.7 12.2 %collective-permute-done.33.refs_3_.refs_7_ = bf16[512,1024]{1,0:T(8,128)(2,1)S(1)} collective-permute-done((bf16[512,1024]{1,0:T(8,128)(2,1)}, bf16[512,1024]{1,0:T(8,128)(2,1)S(1)}, u32[]{:S(2)}, u32[]{:S(2)}) %collective-permute-start.33) | collective-permute-done | bytes 1048608 | tf_op jit(solution)/shard_map/ppermute | solution.py:34
  281.4 28.1 %fc2_pass.1 = (bf16[2048,1024]{1,0:T(8,128)(2,1)}, bf16[512,1024]{1,0:T(8,128)(2,1)}, bf16[512,1024]{1,0:T(8,128)(2,1)}, bf16[512,1024]{1,0:T(8,128)(2,1)}, bf16[512,1024]{1,0:T(8,128)(2,1)}) custom-call(bf16[2048,2048]{1,0:T(8,128)(2,1)} %get-tuple-element.351.hidden_ref, bf16[2048,2048]{1,0:T(8,128)(2,1)} %get-tuple-element.352.cotan_ref, ...), custom_call_target="tpu_custom_call" | custom-call | tf_op jit(solution)/shard_map/fc2_pass/pallas_call | solution.py:558
  309.5 26.8 %back_product.2 = (bf16[1024,2048]{1,0:T(8,128)(2,1)}, bf16[1024,2048]{1,0:T(8,128)(2,1)}) custom-call(s32[17]{0:T(128)} %stack.166.table_ref, bf16[2048,768]{1,0:T(8,128)(2,1)} %get-tuple-element.350.d_proj_ref.first_ref, bf16[2048,1024]{1,0:T(8,128)(2,1)} %get-tuple-element.354.second_ref, bf16[512,1024]{1,0:T(8,128)(2,1)} %copy-done.2, ...), custom_call_target="tpu_custom_call" | custom-call | tf_op jit(solution)/shard_map/back_product/pallas_call | solution.py:605
  340.0 4.4 collective-permute-done.41
  352.7 10.9 %collective-permute-done.38 = bf16[512,1024]{1,0:T(8,128)(2,1)S(1)} collective-permute-done((bf16[512,1024]{1,0:T(8,128)(2,1)S(1)}, bf16[512,1024]{1,0:T(8,128)(2,1)S(1)}, u32[]{:S(2)}, u32[]{:S(2)}) %collective-permute-start.38) | collective-permute-done | bytes 1048608 | tf_op jit(solution)/shard_map/ppermute | solution.py:34
  363.6 22.1 %back_product.3 = (bf16[1024,2048]{1,0:T(8,128)(2,1)}, bf16[1024,2048]{1,0:T(8,128)(2,1)}) custom-call(s32[17]{0:T(128)} %stack.166.table_ref, bf16[2048,256]{1,0:T(8,128)(2,1)} %get-tuple-element.376.context_ref.first_ref, bf16[2048,1024]{1,0:T(8,128)(2,1)} %get-tuple-element.377.second_ref, bf16[512,1024]{1,0:T(8,128)(2,1)} %copy-done.2, ...), custom_call_target="tpu_custom_call" | custom-call | tf_op jit(solution)/shard_map/back_product/pallas_call | solution.py:605
  386.1 5.5 %collective-permute-done.45 = bf16[128,1024]{1,0:T(8,128)(2,1)S(1)} collective-permute-done((bf16[128,1024]{1,0:T(8,128)(2,1)S(1)}, bf16[128,1024]{1,0:T(8,128)(2,1)S(1)}, u32[]{:S(2)}, u32[]{:S(2)}) %collective-permute-start.45) | collective-permute-done | bytes 262176 | tf_op jit(solution)/shard_map/ppermute | solution.py:38
  393.9 4.9 add_add_fusion.1
  415.7 25.0 %collective-permute-done.46 = bf16[512,1024]{1,0:T(8,128)(2,1)} collective-permute-done((bf16[512,1024]{1,0:T(8,128)(2,1)S(1)}, bf16[512,1024]{1,0:T(8,128)(2,1)}, u32[]{:S(2)}, u32[]{:S(2)}) %collective-permute-start.46) | collective-permute-done | bytes 1048608 | tf_op jit(solution)/shard_map/ppermute | solution.py:43
  440.7 6.4 %collective-permute-done.49 = bf16[256,2048]{1,0:T(8,128)(2,1)} collective-permute-done((bf16[256,2048]{1,0:T(8,128)(2,1)}, bf16[256,2048]{1,0:T(8,128)(2,1)}, u32[]{:S(2)}, u32[]{:S(2)}) %collective-permute-start.49) | collective-permute-done | bytes 1048608 | tf_op jit(solution)/shard_map/ppermute | solution.py:34
  469.0 4.3 collective-permute-done.56
  480.1 4.5 add_add_fusion
  489.3 5.6 %add_multiply_fusion.1 = (f32[128,4096]{1,0:T(8,128)}, f32[128,4096]{1,0:T(8,128)}, f32[128,4096]{1,0:T(8,128)}) fusion(bf16[128,4096]{1,0:T(8,128)(2,1)S(1)} %copy-done.11, bf16[128,4096]{1,0:T(8,128)(2,1)S(1)} %constant_dynamic-update-slice_fusion.4, f32[128,4096]{1,0:T(8,128)S(1)} %copy-done.16, f32[128,4096]{1,0:T(8,128)} %param.39), kind=kLoop, calls=%fused_computation.23 | loop fusion | flops 8388608 | bytes 12582912 | tf_op jit(solution)/shard_map/mul | solution.py:642
  498.2 3.8 add_multiply_fusion
  505.0 5.7 %collective-permute-done.64 = bf16[256,2048]{1,0:T(8,128)(2,1)S(1)} collective-permute-done((bf16[256,2048]{1,0:T(8,128)(2,1)}, bf16[256,2048]{1,0:T(8,128)(2,1)S(1)}, u32[]{:S(2)}, u32[]{:S(2)}) %collective-permute-start.64) | collective-permute-done | bytes 1048608 | tf_op jit(solution)/shard_map/ppermute | solution.py:34
  511.3 3.8 fusion.11
  (298 shorter events, 132.2 us)
Async XLA Ops:
  0.7 49.5 %collective-permute-start.3 = (bf16[256,2048]{1,0:T(8,128)(2,1)}, bf16[256,2048]{1,0:T(8,128)(2,1)S(1)}, u32[]{:S(2)}, u32[]{:S(2)}) collective-permute-start(bf16[256,2048]{1,0:T(8,128)(2,1)} %refs_0_), channel_id=1, source_target_pairs={{0,1},{1,0},{2,3},{3,2},{4,5},{5,4},{6,7},{7,6},{8,9},{9,8},{10,11... | collective-permute-start | bytes 3145736 | tf_op jit(solution)/shard_map/ppermute | solution.py:34
  3.7 46.5 %collective-permute-start.4 = (bf16[256,2048]{1,0:T(8,128)(2,1)}, bf16[256,2048]{1,0:T(8,128)(2,1)}, u32[]{:S(2)}, u32[]{:S(2)}) collective-permute-start(bf16[256,2048]{1,0:T(8,128)(2,1)} %refs_0_), channel_id=1, source_target_pairs={{0,8},{8,0},{1,9},{9,1},{2,10},{10,2},{3,11},{11,3},{4,12},{12,4},... | collective-permute-start | bytes 3145736 | tf_op jit(solution)/shard_map/ppermute | solution.py:34
  58.8 47.4 %collective-permute-start.13 = (bf16[512,1024]{1,0:T(8,128)(2,1)S(1)}, bf16[512,1024]{1,0:T(8,128)(2,1)S(1)}, u32[]{:S(2)}, u32[]{:S(2)}) collective-permute-start(bf16[512,1024]{1,0:T(8,128)(2,1)S(1)} %pad_maximum_fusion.refs_16_.refs_0_), channel_id=1, source_target_pairs={{0,16},{16,0},{1,17},{17,1},{2,18},{18,2},{3,19},{19,3},{4,20},{20... | collective-permute-start | bytes 3145736 | tf_op jit(solution)/shard_map/ppermute | solution.py:43
  60.5 45.6 %collective-permute-start.14 = (bf16[512,1024]{1,0:T(8,128)(2,1)S(1)}, bf16[512,1024]{1,0:T(8,128)(2,1)S(1)}, u32[]{:S(2)}, u32[]{:S(2)}) collective-permute-start(bf16[512,1024]{1,0:T(8,128)(2,1)S(1)} %pad_maximum_fusion.refs_16_.refs_0_), channel_id=1, source_target_pairs={{0,4},{4,0},{1,5},{5,1},{2,6},{6,2},{3,7},{7,3},{8,12},{12,8},{9,1... | collective-permute-start | bytes 3145736 | tf_op jit(solution)/shard_map/ppermute | solution.py:34
  62.1 44.1 %collective-permute-start.15 = (bf16[256,2048]{1,0:T(8,128)(2,1)}, bf16[256,2048]{1,0:T(8,128)(2,1)}, u32[]{:S(2)}, u32[]{:S(2)}) collective-permute-start(bf16[256,2048]{1,0:T(8,128)(2,1)} %collective-permute-done.4.refs_2_), channel_id=1, source_target_pairs={{0,1},{1,0},{2,3},{3,2},{4,5},{5,4},{6,7},{7,6},{8,9},{9,8},{10,11... | collective-permute-start | bytes 3145736 | tf_op jit(solution)/shard_map/ppermute | solution.py:34
  62.6 45.4 %collective-permute-start.16 = (bf16[256,2048]{1,0:T(8,128)(2,1)}, bf16[256,2048]{1,0:T(8,128)(2,1)}, u32[]{:S(2)}, u32[]{:S(2)}) collective-permute-start(bf16[256,2048]{1,0:T(8,128)(2,1)} %refs_8_), channel_id=1, source_target_pairs={{0,1},{1,0},{2,3},{3,2},{4,5},{5,4},{6,7},{7,6},{8,9},{9,8},{10,11... | collective-permute-start | bytes 3145736 | tf_op jit(solution)/shard_map/ppermute | solution.py:34
  64.1 45.2 %collective-permute-start.17 = (bf16[256,2048]{1,0:T(8,128)(2,1)}, bf16[256,2048]{1,0:T(8,128)(2,1)}, u32[]{:S(2)}, u32[]{:S(2)}) collective-permute-start(bf16[256,2048]{1,0:T(8,128)(2,1)} %refs_8_), channel_id=1, source_target_pairs={{0,8},{8,0},{1,9},{9,1},{2,10},{10,2},{3,11},{11,3},{4,12},{12,4},... | collective-permute-start | bytes 3145736 | tf_op jit(solution)/shard_map/ppermute | solution.py:34
  109.3 51.7 %collective-permute-start.18 = (bf16[512,1024]{1,0:T(8,128)(2,1)S(1)}, bf16[512,1024]{1,0:T(8,128)(2,1)}, u32[]{:S(2)}, u32[]{:S(2)}) collective-permute-start(bf16[512,1024]{1,0:T(8,128)(2,1)S(1)} %pad_maximum_fusion.1.refs_0_.refs_4_), channel_id=1, source_target_pairs={{0,16},{16,0},{1,17},{17,1},{2,18},{18,2},{3,19},{19,3},{4,20},{20... | collective-permute-start | bytes 3145736 | tf_op jit(solution)/shard_map/ppermute | solution.py:43
  109.8 51.5 %collective-permute-start.19 = (bf16[512,1024]{1,0:T(8,128)(2,1)S(1)}, bf16[512,1024]{1,0:T(8,128)(2,1)S(1)}, u32[]{:S(2)}, u32[]{:S(2)}) collective-permute-start(bf16[512,1024]{1,0:T(8,128)(2,1)S(1)} %pad_maximum_fusion.1.refs_0_.refs_4_), channel_id=1, source_target_pairs={{0,4},{4,0},{1,5},{5,1},{2,6},{6,2},{3,7},{7,3},{8,12},{12,8},{9,1... | collective-permute-start | bytes 3145736 | tf_op jit(solution)/shard_map/ppermute | solution.py:34
  110.3 51.3 %collective-permute-start.20 = (bf16[512,1024]{1,0:T(8,128)(2,1)S(1)}, bf16[512,1024]{1,0:T(8,128)(2,1)S(1)}, u32[]{:S(2)}, u32[]{:S(2)}) collective-permute-start(bf16[512,1024]{1,0:T(8,128)(2,1)S(1)} %collective-permute-done.13.refs_17_.refs_1_), channel_id=1, source_target_pairs={{0,4},{4,0},{1,5},{5,1},{2,6},{6,2},{3,7},{7,3},{8,12},{12,8},{9,1... | collective-permute-start | bytes 3145736 | tf_op jit(solution)/shard_map/ppermute | solution.py:34
  111.9 50.8 %collective-permute-start.21 = (bf16[256,2048]{1,0:T(8,128)(2,1)}, bf16[256,2048]{1,0:T(8,128)(2,1)}, u32[]{:S(2)}, u32[]{:S(2)}) collective-permute-start(bf16[256,2048]{1,0:T(8,128)(2,1)} %collective-permute-done.17.refs_10_), channel_id=1, source_target_pairs={{0,1},{1,0},{2,3},{3,2},{4,5},{5,4},{6,7},{7,6},{8,9},{9,8},{10,11... | collective-permute-start | bytes 3145736 | tf_op jit(solution)/shard_map/ppermute | solution.py:34
  169.8 59.9 %collective-permute-start.31 = (bf16[512,1024]{1,0:T(8,128)(2,1)S(1)}, bf16[512,1024]{1,0:T(8,128)(2,1)}, u32[]{:S(2)}, u32[]{:S(2)}) collective-permute-start(bf16[512,1024]{1,0:T(8,128)(2,1)S(1)} %pad_maximum_fusion.2.refs_0_.refs_4_), channel_id=1, source_target_pairs={{0,16},{16,0},{1,17},{17,1},{2,18},{18,2},{3,19},{19,3},{4,20},{20... | collective-permute-start | bytes 3145736 | tf_op jit(solution)/shard_map/ppermute | solution.py:43
  170.3 59.5 %collective-permute-start.32 = (bf16[512,1024]{1,0:T(8,128)(2,1)S(1)}, bf16[512,1024]{1,0:T(8,128)(2,1)}, u32[]{:S(2)}, u32[]{:S(2)}) collective-permute-start(bf16[512,1024]{1,0:T(8,128)(2,1)S(1)} %pad_maximum_fusion.2.refs_0_.refs_4_), channel_id=1, source_target_pairs={{0,4},{4,0},{1,5},{5,1},{2,6},{6,2},{3,7},{7,3},{8,12},{12,8},{9,1... | collective-permute-start | bytes 3145736 | tf_op jit(solution)/shard_map/ppermute | solution.py:34
  171.1 58.6 %collective-permute-start.30 = (bf16[512,1024]{1,0:T(8,128)(2,1)}, bf16[512,1024]{1,0:T(8,128)(2,1)S(1)}, u32[]{:S(2)}, u32[]{:S(2)}) collective-permute-start(bf16[512,1024]{1,0:T(8,128)(2,1)} %collective-permute-done.18.refs_1_.refs_5_), channel_id=1, source_target_pairs={{0,4},{4,0},{1,5},{5,1},{2,6},{6,2},{3,7},{7,3},{8,12},{12,8},{9,1... | collective-permute-start | bytes 3145736 | tf_op jit(solution)/shard_map/ppermute | solution.py:34
  230.6 46.2 %collective-permute-start.33 = (bf16[512,1024]{1,0:T(8,128)(2,1)}, bf16[512,1024]{1,0:T(8,128)(2,1)S(1)}, u32[]{:S(2)}, u32[]{:S(2)}) collective-permute-start(bf16[512,1024]{1,0:T(8,128)(2,1)} %collective-permute-done.31.refs_1_.refs_5_), channel_id=1, source_target_pairs={{0,4},{4,0},{1,5},{5,1},{2,6},{6,2},{3,7},{7,3},{8,12},{12,8},{9,1... | collective-permute-start | bytes 3145736 | tf_op jit(solution)/shard_map/ppermute | solution.py:34
  276.8 59.5 %collective-permute-start.37 = (bf16[512,1024]{1,0:T(8,128)(2,1)S(1)}, bf16[512,1024]{1,0:T(8,128)(2,1)S(1)}, u32[]{:S(2)}, u32[]{:S(2)}) collective-permute-start(bf16[512,1024]{1,0:T(8,128)(2,1)S(1)} %copy-done.48), channel_id=1, source_target_pairs={{0,4},{4,0},{1,5},{5,1},{2,6},{6,2},{3,7},{7,3},{8,12},{12,8},{9,1... | collective-permute-start | bytes 3145736 | tf_op jit(solution)/shard_map/ppermute | solution.py:34
  277.7 59.1 %collective-permute-start.35 = (bf16[512,1024]{1,0:T(8,128)(2,1)S(1)}, bf16[512,1024]{1,0:T(8,128)(2,1)}, u32[]{:S(2)}, u32[]{:S(2)}) collective-permute-start(bf16[512,1024]{1,0:T(8,128)(2,1)S(1)} %add.527), channel_id=1, source_target_pairs={{0,16},{16,0},{1,17},{17,1},{2,18},{18,2},{3,19},{19,3},{4,20},{20... | collective-permute-start | bytes 3145736 | tf_op jit(solution)/shard_map/ppermute | solution.py:43
  279.9 56.9 %collective-permute-start.36 = (bf16[512,1024]{1,0:T(8,128)(2,1)}, bf16[512,1024]{1,0:T(8,128)(2,1)}, u32[]{:S(2)}, u32[]{:S(2)}) collective-permute-start(bf16[512,1024]{1,0:T(8,128)(2,1)} %get-tuple-element.345), channel_id=1, source_target_pairs={{0,4},{4,0},{1,5},{5,1},{2,6},{6,2},{3,7},{7,3},{8,12},{12,8},{9,1... | collective-permute-start | bytes 3145736 | tf_op jit(solution)/shard_map/ppermute | solution.py:34
  338.0 53.6 %collective-permute-start.39 = (bf16[512,1024]{1,0:T(8,128)(2,1)S(1)}, bf16[512,1024]{1,0:T(8,128)(2,1)}, u32[]{:S(2)}, u32[]{:S(2)}) collective-permute-start(bf16[512,1024]{1,0:T(8,128)(2,1)S(1)} %add.528), channel_id=1, source_target_pairs={{0,16},{16,0},{1,17},{17,1},{2,18},{18,2},{3,19},{19,3},{4,20},{20... | collective-permute-start | bytes 3145736 | tf_op jit(solution)/shard_map/ppermute | solution.py:43
  338.8 52.8 %collective-permute-start.40 = (bf16[512,1024]{1,0:T(8,128)(2,1)}, bf16[512,1024]{1,0:T(8,128)(2,1)}, u32[]{:S(2)}, u32[]{:S(2)}) collective-permute-start(bf16[512,1024]{1,0:T(8,128)(2,1)} %get-tuple-element.373), channel_id=1, source_target_pairs={{0,4},{4,0},{1,5},{5,1},{2,6},{6,2},{3,7},{7,3},{8,12},{12,8},{9,1... | collective-permute-start | bytes 3145736 | tf_op jit(solution)/shard_map/ppermute | solution.py:34
  347.2 44.4 %collective-permute-start.42 = (bf16[256,2048]{1,0:T(8,128)(2,1)}, bf16[256,2048]{1,0:T(8,128)(2,1)}, u32[]{:S(2)}, u32[]{:S(2)}) collective-permute-start(bf16[256,2048]{1,0:T(8,128)(2,1)} %dynamic-slice_add_fusion.3), channel_id=1, source_target_pairs={{0,1},{1,0},{2,3},{3,2},{4,5},{5,4},{6,7},{7,6},{8,9},{9,8},{10,11... | collective-permute-start | bytes 3145736 | tf_op jit(solution)/shard_map/ppermute | solution.py:34
  392.4 48.2 %collective-permute-start.46 = (bf16[512,1024]{1,0:T(8,128)(2,1)S(1)}, bf16[512,1024]{1,0:T(8,128)(2,1)}, u32[]{:S(2)}, u32[]{:S(2)}) collective-permute-start(bf16[512,1024]{1,0:T(8,128)(2,1)S(1)} %add.529), channel_id=1, source_target_pairs={{0,16},{16,0},{1,17},{17,1},{2,18},{18,2},{3,19},{19,3},{4,20},{20... | collective-permute-start | bytes 3145736 | tf_op jit(solution)/shard_map/ppermute | solution.py:43
  392.5 48.1 %collective-permute-start.47 = (bf16[512,1024]{1,0:T(8,128)(2,1)}, bf16[512,1024]{1,0:T(8,128)(2,1)}, u32[]{:S(2)}, u32[]{:S(2)}) collective-permute-start(bf16[512,1024]{1,0:T(8,128)(2,1)} %get-tuple-element.393), channel_id=1, source_target_pairs={{0,4},{4,0},{1,5},{5,1},{2,6},{6,2},{3,7},{7,3},{8,12},{12,8},{9,1... | collective-permute-start | bytes 3145736 | tf_op jit(solution)/shard_map/ppermute | solution.py:34
  399.3 47.7 %collective-permute-start.49 = (bf16[256,2048]{1,0:T(8,128)(2,1)}, bf16[256,2048]{1,0:T(8,128)(2,1)}, u32[]{:S(2)}, u32[]{:S(2)}) collective-permute-start(bf16[256,2048]{1,0:T(8,128)(2,1)} %get-tuple-element.487), channel_id=1, source_target_pairs={{0,8},{8,0},{1,9},{9,1},{2,10},{10,2},{3,11},{11,3},{4,12},{12,4},... | collective-permute-start | bytes 3145736 | tf_op jit(solution)/shard_map/ppermute | solution.py:34
  (91 other events, 1758.7 us)
